TPU v7x, 32 devices: a whole 2x2x4 slice. The times are simulated.
32 devices in a mesh: tile: 8 (over z, y), depth: 4 (over x, core).
Axes of the slice: x: 2, y: 2, z: 4, core: 2. Of those that a mesh axis runs over, the one named last changes fastest.
Arguments:
- owned_blocks: bfloat16 [4, 512, 32768], P('depth', 'tile'), may hold values from -6 to 6
- slot_counts: int32 [4, 8], P('depth'), may hold values from 1 to 64, 256 in all within a row
- brick_order: int32 [4, 8], P('depth'), may hold values from 0 to 7, each once within a row
- view_flip: int32 [8], replicated, may hold values from 0 to 1
- tf_centers: float32 [8], replicated, may hold values from -2.5 to 2.5
- tf_amps: float32 [4, 8], replicated, may hold values from -6 to 6
Outputs:
- image: float32 [4, 128, 1024], P(None, 'depth', 'tile')
Inputs may be any that keep to these rules, and one draw needn't show every extreme that they name: `slot_counts`: every row sums to 256, and some entry of every row equals 64. `brick_order`: every row holds each of 0 to 7 once.
All inputs are finite; a program needn't handle non-finite values.
Results may differ from a plain program's by a relative error of at most 0.0003.
Values may be sent and summed in bfloat16 or wider, within the bound.
No kernel may reach another device: no remote copies, remote signals or barrier semaphores. Data moves between devices by JAX's collectives and lax.ppermute only.
A program may use at most 64 MiB of HBM per device.

v0:
```python
import jax
import jax.numpy as jnp
from jax import lax
from jax.sharding import PartitionSpec as P

BLOCK = 32
BX = 4
BY = 4
DB = 2
KNOTS = 8


bump_scale = 4.0


def swapped(block, axis, bit):
    count = lax.axis_size(axis)
    route = []
    for low in range(count):
        high = low | 1 << bit
        if high != low and high < count:
            route += [(low, high), (high, low)]
    return lax.ppermute(block, axis, route)


def select_entry(table, index, tile_lane):
    return jnp.sum(jnp.where(tile_lane == index, table, 0))


def over_blend(nearer, farther, chan_axis):
    coverage = lax.slice_in_dim(nearer, 3, 4, axis=chan_axis)
    return nearer + (1.0 - coverage) * farther


def march_blocks(blocks, flip_rows, tf_centers, tf_amps, step_size):
    block_count = blocks.shape[0]
    values = blocks.reshape(block_count, BLOCK, BLOCK * BLOCK).astype(jnp.float32)
    fields = [jnp.zeros_like(values) for channel in range(4)]
    for knot_index in range(KNOTS):
        bump_term = jnp.exp(-bump_scale * jnp.square(values - tf_centers[knot_index]))
        fields = [
            fields[channel] + tf_amps[channel, knot_index] * bump_term for channel in range(4)
        ]
    extinction = jax.nn.softplus(fields[3])
    opacity_step = 1.0 - jnp.exp(-step_size * extinction)
    depth_row = lax.broadcasted_iota(jnp.int32, (BLOCK, BLOCK), 0)
    depth_col = lax.broadcasted_iota(jnp.int32, (BLOCK, BLOCK), 1)
    lower_mask = (depth_col < depth_row).astype(jnp.float32)
    upper_mask = (depth_col > depth_row).astype(jnp.float32)
    weights = jnp.where(flip_rows[:, None, None] == 1, upper_mask[None], lower_mask[None])
    before = jnp.einsum("nzw,nwp->nzp", weights, extinction, precision=lax.Precision.HIGHEST)
    passed = jnp.exp(-step_size * before) * opacity_step
    colors = [jnp.sum(passed * jax.nn.sigmoid(fields[channel]), axis=1) for channel in range(3)]
    opacity = 1.0 - jnp.exp(-step_size * jnp.sum(extinction, axis=1))
    return jnp.stack(colors + [opacity], axis=1)


def body(owned_blocks, slot_counts, brick_order, view_flip, tf_centers, tf_amps):
    tile_count = lax.axis_size("tile")
    depth_count = lax.axis_size("depth")
    mine_tile = lax.axis_index("tile")
    depth_index = lax.axis_index("depth")
    step_size = 1.5 / (depth_count * DB * BLOCK)
    tile_lane = jnp.arange(tile_count, dtype=jnp.int32)
    counts = slot_counts[0]
    order_row = brick_order[0]
    starts = jnp.cumsum(counts) - counts
    start_mine = select_entry(starts, mine_tile, tile_lane)
    position = jnp.sum(
        jnp.where(order_row[None, :] == tile_lane[:, None], tile_lane[None, :], 0), axis=1
    )
    position_mine = select_entry(position, mine_tile, tile_lane)
    flip_mine = select_entry(view_flip, mine_tile, tile_lane)
    slot_total = owned_blocks.shape[1]
    capacity = slot_total // tile_count
    brick_total = slot_total // 2
    offsets = jnp.mod(position - start_mine, tile_count)
    send_slots = (
        offsets[:, None] + tile_count * jnp.arange(capacity, dtype=jnp.int32)[None, :]
    ).reshape(-1)
    wanted = jnp.arange(brick_total, dtype=jnp.int32) * tile_count + position_mine
    owner_index = jnp.sum((starts[None, :] <= wanted[:, None]).astype(jnp.int32), axis=1) - 1
    owner_start = jnp.sum(
        jnp.where(tile_lane[None, :] == owner_index[:, None], starts[None, :], 0), axis=1
    )
    row_index = owner_index * capacity + (wanted - owner_start) // tile_count
    outgoing = jnp.take(owned_blocks[0], send_slots, axis=0)
    arrived = lax.all_to_all(outgoing, "tile", split_axis=0, concat_axis=0, tiled=True)
    brick_blocks = jnp.take(arrived, row_index, axis=0)
    flip_rows = jnp.zeros((brick_total,), jnp.int32) + flip_mine
    partial_value = march_blocks(brick_blocks, flip_rows, tf_centers, tf_amps, step_size)
    layers = partial_value.reshape(DB, BY, BX, 4, BLOCK * BLOCK)
    nearest_first = jnp.where(flip_mine == 1, layers[::-1], layers)
    combined = nearest_first[DB - 1]
    combined = over_blend(nearest_first[0], combined, 2)
    tile_image = (
        combined.reshape(BY, BX, 4, BLOCK, BLOCK)
        .transpose(2, 0, 3, 1, 4)
        .reshape(4, BY * BLOCK, BX * BLOCK)
    )
    levels = depth_count.bit_length() - 1
    row_share = tile_image.shape[1] // depth_count
    width = tile_image.shape[2]
    current = tile_image.reshape((4,) + (2,) * levels + (row_share, width))
    for bit_index in range(levels):
        split_axis = 1 + (levels - 1 - bit_index)
        lower_half = lax.slice_in_dim(current, 0, 1, axis=split_axis)
        upper_half = lax.slice_in_dim(current, 1, 2, axis=split_axis)
        high_side = depth_index >> bit_index & 1
        kept_half = jnp.where(high_side == 1, upper_half, lower_half)
        given_half = jnp.where(high_side == 1, lower_half, upper_half)
        other_half = swapped(given_half, "depth", bit_index)
        mine_front = high_side == flip_mine
        current = jnp.where(
            mine_front, over_blend(kept_half, other_half, 0), over_blend(other_half, kept_half, 0)
        )
    result = current.reshape(4, row_share, width)
    return result


def solution(mesh):
    in_specs = (P("depth", "tile", None), P("depth", None), P("depth", None), P(), P(), P())
    out_specs = P(None, "depth", "tile")
    return jax.shard_map(body, mesh=mesh, in_specs=in_specs, out_specs=out_specs, check_vma=False)
```

profile of v0, /device:TPU:0, one launch (start us, length us, event | category | flops | bytes accessed | tf_op | source)
XLA Modules:
  0.0 229.7 jit_solution(1593695551208081773)
XLA Ops:
  0.0 0.8 select_reduce_fusion.1
  0.8 0.8 reduce-window.4
  1.6 1.3 fusion.112
  2.9 1.2 select_reduce_fusion.2
  4.2 0.1 broadcast_add_fusion
  4.3 0.1 compare_and_fusion
  4.3 0.1 add.265
  4.4 11.5 %gather_fusion = bf16[64,32768]{1,0:T(8,128)(2,1)} fusion(bf16[64,32768]{1,0:T(8,128)(2,1)} %bitcast.99, s32[1024]{0:T(1024)S(1)} %pad_clamp_fusion.1), kind=kCustom, calls=%fused_computation | custom fusion | bytes 8388864 | tf_op jit(solution)/shard_map/jit(_take)/gather | solution.py:87
  15.9 4.6 %bitcast_select_fusion = bf16[8,8,32768]{2,1,0:T(8,128)(2,1)} fusion(bf16[64,32768]{1,0:T(8,128)(2,1)} %gather_fusion, pred[8,8]{1,0:T(8,128)(4,1)S(1)} %compare_and_fusion), kind=kLoop, calls=%fused_computation.110 | loop fusion | flops 2097152 | bytes 8388672 | tf_op jit(solution)/shard_map/jit(_take)/select_n | solution.py:87
  20.5 0.0 copy-start.4
  20.5 0.0 copy-start.3
  20.5 0.0 copy-start.2
  20.5 7.4 %all-to-all-start = ((bf16[8,8,32768]{2,1,0:T(8,128)(2,1)}), bf16[8,8,32768]{2,1,0:T(8,128)(2,1)}, u32[]{:S(2)}, u32[]{:S(2)}) async-start(bf16[8,8,32768]{2,1,0:T(8,128)(2,1)} %bitcast_select_fusion), calls=%async_computation | async-start | bytes 8388608 | tf_op jit(solution)/shard_map/all_to_all | solution.py:88
  29.8 0.6 multiply_add_fusion
  30.4 0.0 copy-done.4
  30.4 0.1 convert_reduce_fusion
  30.5 0.1 select_reduce_fusion
  30.6 0.6 fusion.110
  31.2 0.0 copy-done.3
  31.2 0.7 fusion.117
  31.9 0.0 copy-done.2
  31.9 0.7 fusion.116
  32.6 0.7 fusion.115
  33.3 0.6 compare_and_fusion.1
  33.9 87.3 %all-to-all-done = bf16[8,8,32768]{2,1,0:T(8,128)(2,1)} async-done(((bf16[8,8,32768]{2,1,0:T(8,128)(2,1)}), bf16[8,8,32768]{2,1,0:T(8,128)(2,1)}, u32[]{:S(2)}, u32[]{:S(2)}) %all-to-all-start) | async-done | bytes 4194336 | tf_op jit(solution)/shard_map/all_to_all | solution.py:88
  121.2 6.4 %gather_fusion.1 = bf16[32,32768]{1,0:T(8,128)(2,1)S(1)} fusion(bf16[64,32768]{1,0:T(8,128)(2,1)} %bitcast.10, s32[1024]{0:T(1024)S(1)} %pad_clamp_fusion), kind=kCustom, calls=%fused_computation.1 | custom fusion | bytes 4194432 | tf_op jit(solution)/shard_map/jit(_take)/gather | solution.py:89
  127.6 1.2 copy.9
  128.8 0.0 copy-start
  128.8 21.6 %fusion.114 = (f32[32,1024]{1,0:T(8,128)S(1)}, f32[32,32,1024]{2,1,0:T(8,128)}) fusion(f32[]{:T(128)} %bitcast.28, f32[]{:T(128)} %bitcast.27, f32[]{:T(128)} %bitcast.26, f32[]{:T(128)} %bitcast.25, f32[]{:T(128)} %bitcast.24, f32[]{:T(128)} %bitcast.23, f32[]{:T(128)} %bitcast.22, f32[]{:T(128)} %bitcast.21, f32[]{:T(128)} %bitcast.20, f32[]{:T(128)} %bitcast.19, ...), kind=kLoop, calls=%fused_computation.182 | loop fusion | flops 50298880 | bytes 6422624 | tf_op jit(solution)/shard_map/reduce_sum | solution.py:54
  150.4 0.0 copy-done
  150.4 0.2 sub.156
  150.6 0.0 copy-start.1
  150.6 28.2 %fusion.99 = (f32[32,1024]{1,0:T(8,128)S(1)}, f32[32,32,1024]{2,1,0:T(8,128)}) fusion(f32[]{:T(128)} %bitcast.52, f32[]{:T(128)} %bitcast.51, f32[]{:T(128)} %bitcast.50, f32[]{:T(128)} %bitcast.49, f32[]{:T(128)} %bitcast.48, f32[]{:T(128)} %bitcast.47, f32[]{:T(128)} %bitcast.46, f32[]{:T(128)} %bitcast.45, f32[]{:T(128)} %bitcast.28, f32[]{:T(128)} %bitcast.26, ...), kind=kOutput, calls=%fused_computation.112 | convolution fusion | flops 455049216 | bytes 10621024 | tf_op jit(solution)/shard_map/nzw,nwp->nzp/dot_general | solution.py:51
  178.8 0.2 stack.15
  179.0 0.0 copy-done.1
  179.0 20.2 %fusion.100 = f32[32,1024]{1,0:T(8,128)S(1)} fusion(f32[32,32,1024]{2,1,0:T(8,128)} %get-tuple-element.57, f32[]{:T(128)} %bitcast.44, f32[]{:T(128)} %bitcast.43, f32[]{:T(128)} %bitcast.42, f32[]{:T(128)} %bitcast.41, f32[]{:T(128)} %bitcast.40, f32[]{:T(128)} %bitcast.39, f32[]{:T(128)} %bitcast.38, f32[]{:T(128)} %bitcast.37, f32[]{:T(128)} %bitcast.28, ...), kind=kLoop, calls=%fused_computation.113 | loop fusion | flops 48201728 | bytes 6422624 | tf_op jit(solution)/shard_map/reduce_sum | solution.py:53
  199.2 0.2 stack.14
  199.3 20.3 %fusion.101 = f32[32,1024]{1,0:T(8,128)S(1)} fusion(f32[32,32,1024]{2,1,0:T(8,128)} %get-tuple-element.57, f32[]{:T(128)} %bitcast.36, f32[]{:T(128)} %bitcast.35, f32[]{:T(128)} %bitcast.34, f32[]{:T(128)} %bitcast.33, f32[]{:T(128)} %bitcast.32, f32[]{:T(128)} %bitcast.31, f32[]{:T(128)} %bitcast.30, f32[]{:T(128)} %bitcast.29, f32[]{:T(128)} %bitcast.28, ...), kind=kLoop, calls=%fused_computation.114 | loop fusion | flops 48201728 | bytes 6422624 | tf_op jit(solution)/shard_map/reduce_sum | solution.py:53
  219.7 0.2 stack.13
  219.8 0.5 pad_maximum_fusion
  220.4 0.1 reverse_select_fusion
  220.5 0.1 slice_bitcast_fusion
  220.6 0.4 squeeze.176
  221.0 0.4 squeeze.178
  221.4 0.2 fusion.103
  221.6 0.1 mul.425
  221.7 0.3 add_bitcast_fusion
  222.0 0.7 copy.8
  222.7 0.5 reshape_reshape.3
  223.2 0.1 collective-permute-start
  223.3 1.3 collective-permute-done
  224.7 1.6 collective-permute-start.1
  226.2 2.8 %collective-permute-done.1 = f32[4,1,1,32,128]{4,3,2,1,0:T(8,128)S(1)} collective-permute-done((f32[4,1,1,32,128]{4,3,2,1,0:T(8,128)S(1)}, f32[4,1,1,32,128]{4,3,2,1,0:T(8,128)S(1)}, u32[]{:S(2)}, u32[]{:S(2)}) %collective-permute-start.1) | collective-permute-done | bytes 65568 | tf_op jit(solution)/shard_map/ppermute | solution.py:23
  229.0 0.6 select_bitcast_fusion
  (15 shorter events, 0.2 us)
Async XLA Ops:
  20.5 9.9 %copy-start.4 = (s32[1,8]{1,0:T(1,128)S(1)}, s32[1,8]{1,0:T(1,128)}, u32[]{:S(2)}) copy-start(s32[1,8]{1,0:T(1,128)} %param.7) | copy-start | bytes 100
  20.5 10.7 %copy-start.3 = (f32[8]{0:T(128)S(1)}, f32[8]{0:T(128)}, u32[]{:S(2)}) copy-start(f32[8]{0:T(128)} %param.10) | copy-start | bytes 100
  20.5 11.4 %copy-start.2 = (f32[4,8]{1,0:T(4,128)S(1)}, f32[4,8]{1,0:T(4,128)}, u32[]{:S(2)}) copy-start(f32[4,8]{1,0:T(4,128)} %param.11) | copy-start | bytes 388
  20.5 100.7 %all-to-all-start = ((bf16[8,8,32768]{2,1,0:T(8,128)(2,1)}), bf16[8,8,32768]{2,1,0:T(8,128)(2,1)}, u32[]{:S(2)}, u32[]{:S(2)}) async-start(bf16[8,8,32768]{2,1,0:T(8,128)(2,1)} %bitcast_select_fusion), calls=%async_computation | async-start | bytes 8388608 | tf_op jit(solution)/shard_map/all_to_all | solution.py:88
  128.8 21.6 %copy-start = (bf16[4,8,32,1024]{3,2,1,0:T(8,128)(2,1)}, bf16[4,8,32,1024]{3,2,1,0:T(8,128)(2,1)S(1)}, u32[]{:S(2)}) copy-start(bf16[4,8,32,1024]{3,2,1,0:T(8,128)(2,1)S(1)} %copy.9) | copy-start | bytes 6291460
  150.6 28.4 %copy-start.1 = (bf16[4,8,32,1024]{3,2,1,0:T(8,128)(2,1)S(1)}, bf16[4,8,32,1024]{3,2,1,0:T(8,128)(2,1)}, u32[]{:S(2)}) copy-start(bf16[4,8,32,1024]{3,2,1,0:T(8,128)(2,1)} %copy-done) | copy-start | bytes 6291460
  223.2 1.4 collective-permute-start
  224.7 4.3 %collective-permute-start.1 = (f32[4,1,1,32,128]{4,3,2,1,0:T(8,128)S(1)}, f32[4,1,1,32,128]{4,3,2,1,0:T(8,128)S(1)}, u32[]{:S(2)}, u32[]{:S(2)}) collective-permute-start(f32[4,1,1,32,128]{4,3,2,1,0:T(8,128)S(1)} %get-tuple-element.13), channel_id=1, source_target_pairs={{0,2},{2,0},{1,3},{3,1},{4,6},{6,4},{5,7},{7,5},{8,10},{10,8},{9,1... | collective-permute-start | bytes 196616 | tf_op jit(solution)/shard_map/ppermute | solution.py:23
where the time goes:
time: 231 us; the launch traced here: 230 us
  waiting for transfers between devices  91.4 us (40%)
  other arithmetic  74.9 us (32%)
  matrix products  28.2 us (12%)
  local copies, waits for them, and re-layouts  24 us (10%)
  starting transfers between devices  9.07 us (4%)
    all_to_all x1, waiting for transfers between devices, body(): lax.all_to_all(outgoing, 'tile', split_axis=0, concat_axis=0, tiled=True)  87.3 us
    reduce_sum x2, other arithmetic, march_blocks(): jnp.sum(passed * jax.nn.sigmoid(fields[channel]), axis=1)  40.5 us
    dot_general x1, matrix products, march_blocks(): jnp.einsum('nzw,nwp->nzp', weights, extinction, precision=lax.Precision.H...  28.2 us
    reduce_sum x1, other arithmetic, march_blocks(): opacity = 1.0 - jnp.exp(-step_size * jnp.sum(extinction, axis=1))  21.6 us
    gather x1, local copies, waits for them, and re-layouts, body(): outgoing = jnp.take(owned_blocks[0], send_slots, axis=0)  11.5 us
    all_to_all x1, starting transfers between devices, body(): lax.all_to_all(outgoing, 'tile', split_axis=0, concat_axis=0, tiled=True)  7.44 us
    gather x1, local copies, waits for them, and re-layouts, body(): brick_blocks = jnp.take(arrived, row_index, axis=0)  6.38 us
  transfers between devices with their start and end apart: 3, of which 3 were waited for; matrix products, arithmetic and copies ran while one was open for 2% of the time, Pallas kernels for 0%

commit v1 on v0

v1 whole, which is shorter than its diff:
```python
import functools
import math

import jax
import jax.numpy as jnp
from jax import lax
from jax.experimental import pallas as pl
from jax.experimental.pallas import tpu as pltpu
from jax.sharding import PartitionSpec as P

BLOCK = 32
BX = 4
BY = 4
DB = 2
KNOTS = 8
PIXELS = BLOCK * BLOCK
LANES = 128
TILES = PIXELS // LANES
BUMP_SCALE = 4.0
LOG2E = math.log2(math.e)
ROOT = math.sqrt(BUMP_SCALE * LOG2E)
CODE_TOP = 65535.0
CODE_MID = 32767.5
WIDE = 2


def exclusive_start(counts_ref, index, tile_count):
    start = jnp.int32(0)
    for i in range(tile_count):
        start = start + jnp.where(i < index, counts_ref[i], 0)
    return start


def position_of(order_ref, tile, tile_count):
    position = jnp.int32(0)
    for i in range(tile_count):
        position = position + jnp.where(order_ref[i] == tile, i, 0)
    return position


def encode(image):
    root = jnp.sqrt(jnp.sqrt(jnp.maximum(image, 0.0)))
    code = jnp.round(jnp.minimum(root, 1.0) * CODE_TOP - CODE_MID)
    return code.astype(jnp.int32).astype(jnp.int16)


def decode(code):
    root = (code.astype(jnp.int32).astype(jnp.float32) + CODE_MID) * (1.0 / CODE_TOP)
    square = root * root
    return square * square


def march_kernel(step_size, tile_count, relative, *refs):
    counts_ref, order_ref, flip_ref, me_ref, center_ref, amp_ref, cells_ref = refs[:7]
    outs = refs[7:7 + relative]
    coef_ref, stage_ref = refs[7 + relative:]
    step = pl.program_id(0)
    me = me_ref[0]
    start = exclusive_start(counts_ref, me, tile_count)
    live = counts_ref[me]

    @pl.when(step == 0)
    def _():
        w = center_ref[...] * ROOT
        folded = amp_ref[...] * jnp.exp2(-w * w)
        for k in range(KNOTS):
            coef_ref[k] = jnp.broadcast_to(2.0 * w[:, k:k + 1], (8, LANES))
            for c in range(4):
                scale = LOG2E if c == 3 else 0.5
                coef_ref[KNOTS + 4 * k + c] = jnp.broadcast_to(
                    folded[c:c + 1, k:k + 1] * scale, (8, LANES)
                )

    @pl.when(step * tile_count < live)
    def _():
        row = lax.broadcasted_iota(jnp.int32, (8, LANES), 0)
        for half in range(tile_count // 8):
            flip = jnp.zeros((8, LANES), jnp.int32)
            for s in range(8):
                tile = order_ref[lax.rem(start + half * 8 + s, tile_count)]
                flip = jnp.where(row == s, flip_ref[tile], flip)
            down = flip == 1
            signed_step = jnp.where(down, step_size * LOG2E, -step_size * LOG2E)

            def columns(group, carry, half=half, down=down, signed_step=signed_step):
                base = group * (WIDE * LANES)

                def depth(z, state):
                    lane = pl.multiple_of(z * PIXELS + base, LANES)
                    raw = cells_ref[half * 8:half * 8 + 8, pl.ds(lane, WIDE * LANES)]
                    values = raw.astype(jnp.float32) * ROOT
                    after = []
                    for j in range(WIDE):
                        v = values[:, j * LANES:(j + 1) * LANES]
                        total, seen, reds, greens, blues = state[j]
                        fields = [None] * 4
                        for k in range(KNOTS):
                            bump = jnp.exp2(v * (coef_ref[k] - v))
                            for c in range(4):
                                term = coef_ref[KNOTS + 4 * k + c] * bump
                                fields[c] = term if k == 0 else fields[c] + term
                        total = total + jnp.log(1.0 + jnp.exp2(fields[3]))
                        now = jnp.exp2(signed_step * total)
                        weight = now - seen
                        after.append((
                            total,
                            now,
                            reds + weight * jnp.tanh(fields[0]),
                            greens + weight * jnp.tanh(fields[1]),
                            blues + weight * jnp.tanh(fields[2]),
                        ))
                    return tuple(after)

                zero = jnp.zeros((8, LANES), jnp.float32)
                first = tuple((zero, zero + 1.0, zero, zero, zero) for j in range(WIDE))
                last = lax.fori_loop(0, BLOCK, depth, first)
                for j in range(WIDE):
                    total, seen, reds, greens, blues = last[j]
                    passed = jnp.exp2(total * (-step_size * LOG2E))
                    factor = jnp.where(down, 0.5 * passed, -0.5)
                    spread = seen - 1.0
                    rows = pl.ds(group * WIDE + j, 8, stride=TILES)
                    for c, color in enumerate((reds, greens, blues)):
                        stage_ref[half, c, rows, :] = factor * (spread + color)
                    stage_ref[half, 3, rows, :] = 1.0 - passed
                return carry

            lax.fori_loop(0, TILES // WIDE, columns, 0)
        for r in range(relative):
            tile = lax.rem(me + r, tile_count)
            slot = lax.rem(position_of(order_ref, tile, tile_count) - start + tile_count * 64, tile_count)
            rows = pl.ds(pl.multiple_of(lax.rem(slot, 8) * TILES, TILES), TILES)
            for c in range(4):
                outs[r][0, c] = encode(stage_ref[slot // 8, c, rows, :])


def march(counts, order, flip, me, centers, amps, cells, step_size):
    tile_count = counts.shape[0]
    slots = cells.shape[0]
    capacity = slots // tile_count
    scalar = pl.BlockSpec(memory_space=pltpu.SMEM)
    whole = lambda shape: pl.BlockSpec(shape, lambda m: (0,) * len(shape))
    block = pl.BlockSpec((1, 4, TILES, LANES), lambda m: (m, 0, 0, 0))
    return pl.pallas_call(
        functools.partial(march_kernel, step_size, tile_count, tile_count),
        grid=(capacity,),
        in_specs=[scalar] * 4 + [
            whole((1, KNOTS)),
            whole((4, KNOTS)),
            pl.BlockSpec((tile_count, cells.shape[1]), lambda m: (m, 0)),
        ],
        out_specs=[block] * tile_count,
        out_shape=[jax.ShapeDtypeStruct((capacity, 4, TILES, LANES), jnp.int16)] * tile_count,
        scratch_shapes=[
            pltpu.VMEM((KNOTS * 5, 8, LANES), jnp.float32),
            pltpu.VMEM((tile_count // 8, 4, 8 * TILES, LANES), jnp.float32),
        ],
        name="march",
    )(counts, order, flip, me, centers.reshape(1, KNOTS), amps, cells)


def over(nearer, farther, uncovered):
    return nearer + uncovered * farther


def gather_kernel(tile_count, capacity, *refs):
    counts_ref, order_ref, flip_ref, me_ref = refs[:4]
    arrived = refs[4:4 + tile_count]
    out_ref, brick_ref = refs[4 + tile_count:]
    me = me_ref[0]
    position = position_of(order_ref, me, tile_count)
    for r in range(tile_count):
        owner = lax.rem(me - r + tile_count, tile_count)
        start = exclusive_start(counts_ref, owner, tile_count)
        offset = lax.rem(position - start + tile_count * 64, tile_count)
        level = (start + offset - position) // tile_count
        held = (counts_ref[owner] - offset + tile_count - 1) // tile_count

        def place(m, carry, r=r, level=level):
            for c in range(4):
                brick_ref[level + m, c] = decode(arrived[r][m, c])
            return carry

        lax.fori_loop(0, held, place, 0)
    flip = flip_ref[me] == 1
    lane = lax.broadcasted_iota(jnp.int32, (TILES, LANES), 1) // BLOCK
    per_row = LANES // BLOCK
    for by in range(BY):
        images = []
        for bx in range(BX):
            layers = [(bz * BY + by) * BX + bx for bz in range(DB)]
            parts = None
            for n in range(DB):
                index = jnp.where(flip, layers[n], layers[DB - 1 - n])
                new = [brick_ref[index, c] for c in range(4)]
                if parts is None:
                    parts = new
                else:
                    uncovered = 1.0 - new[3]
                    parts = [new[c] + uncovered * parts[c] for c in range(4)]
            images.append(parts)
        for c in range(4):
            for s in range(per_row):
                line = None
                for bx in range(BX):
                    turn = (bx - s) * BLOCK % LANES
                    moved = images[bx][c]
                    if turn:
                        moved = pltpu.roll(moved, turn, 1)
                    line = moved if line is None else jnp.where(lane == bx, moved, line)
                out_ref[c, pl.ds(by * BLOCK + s, TILES, stride=per_row), :] = line


def gather(counts, order, flip, me, arrived):
    tile_count = counts.shape[0]
    capacity = arrived[0].shape[0]
    scalar = pl.BlockSpec(memory_space=pltpu.SMEM)
    vmem = pl.BlockSpec(memory_space=pltpu.VMEM)
    return pl.pallas_call(
        functools.partial(gather_kernel, tile_count, capacity),
        in_specs=[scalar] * 4 + [vmem] * tile_count,
        out_specs=vmem,
        out_shape=jax.ShapeDtypeStruct((4, BY * BLOCK, BX * BLOCK), jnp.float32),
        scratch_shapes=[pltpu.VMEM((DB * BY * BX, 4, TILES, LANES), jnp.float32)],
        name="gather",
    )(counts, order, flip, me, *arrived)


def over_blend(nearer, farther, chan_axis):
    coverage = lax.slice_in_dim(nearer, 3, 4, axis=chan_axis)
    return nearer + (1.0 - coverage) * farther


def swapped(block, axis, bit):
    count = lax.axis_size(axis)
    return lax.ppermute(block, axis, [(i, i ^ 1 << bit) for i in range(count)])


def body(owned_blocks, slot_counts, brick_order, view_flip, tf_centers, tf_amps):
    tile_count = lax.axis_size("tile")
    depth_count = lax.axis_size("depth")
    depth_index = lax.axis_index("depth")
    step_size = 1.5 / (depth_count * DB * BLOCK)
    me = lax.axis_index("tile").astype(jnp.int32).reshape(1)
    counts, order = slot_counts[0], brick_order[0]
    sent = march(counts, order, view_flip, me, tf_centers, tf_amps, owned_blocks[0], step_size)
    arrived = [sent[0]]
    for r in range(1, tile_count):
        route = [(i, (i + r) % tile_count) for i in range(tile_count)]
        arrived.append(lax.ppermute(sent[r], "tile", route))
    tile_image = gather(counts, order, view_flip, me, arrived)
    flip_mine = jnp.sum(jnp.where(jnp.arange(tile_count, dtype=jnp.int32) == me[0], view_flip, 0))
    levels = depth_count.bit_length() - 1
    row_share = tile_image.shape[1] // depth_count
    width = tile_image.shape[2]
    current = tile_image.reshape((4,) + (2,) * levels + (row_share, width))
    for bit_index in range(levels):
        split_axis = 1 + (levels - 1 - bit_index)
        lower_half = lax.slice_in_dim(current, 0, 1, axis=split_axis)
        upper_half = lax.slice_in_dim(current, 1, 2, axis=split_axis)
        high_side = depth_index >> bit_index & 1
        kept_half = jnp.where(high_side == 1, upper_half, lower_half)
        given_half = jnp.where(high_side == 1, lower_half, upper_half)
        other_half = swapped(given_half, "depth", bit_index)
        mine_front = high_side == flip_mine
        current = jnp.where(
            mine_front, over_blend(kept_half, other_half, 0), over_blend(other_half, kept_half, 0)
        )
    return current.reshape(4, row_share, width)


def solution(mesh):
    in_specs = (P("depth", "tile", None), P("depth", None), P("depth", None), P(), P(), P())
    out_specs = P(None, "depth", "tile")
    return jax.shard_map(body, mesh=mesh, in_specs=in_specs, out_specs=out_specs, check_vma=False)
```

time: 231 us -> 92.9 us (0.40)
  waiting for transfers between devices: 91.4 us -> 4.9 us
  other arithmetic: 74.9 us -> 1.33 us
  starting transfers between devices: 9.07 us -> 59.1 us
  matrix products: 28.2 us -> 0 us
  Pallas kernels: 0 us -> 23.8 us
  local copies, waits for them, and re-layouts: 24 us -> 1.61 us
    all_to_all x1 -> x0, waiting for transfers between devices: 87.3 us -> none  [body(): lax.all_to_all(outgoing, 'tile', split_axis=0, concat_axis=0, tiled=True)]
    reduce_sum x8 -> x1, other arithmetic: 65.7 us -> 0.6 us  [body(): jnp.sum(jnp.where(jnp.arange(tile_count, dtype=jnp.int32) == me[0], view_...]
    ppermute x2 -> x9, starting transfers between devices: 1.63 us -> 59.1 us  [the longest x7 56.9 us: body(): arrived.append(lax.ppermute(sent[r], 'tile', route))]
    dot_general x1 -> x0, matrix products: 28.2 us -> none  [march_blocks(): jnp.einsum('nzw,nwp->nzp', weights, extinction, precision=lax.Precision.H...]
    pallas_call x0 -> x2, Pallas kernels: none -> 23.8 us  [the longest x1 21.3 us: march(): pl.pallas_call(functools.partial(march_kernel, step_size, tile_count, til...]
    gather x2 -> x0, local copies, waits for them, and re-layouts: 17.9 us -> none  [the longest x1 11.5 us: body(): outgoing = jnp.take(owned_blocks[0], send_slots, axis=0)]
    all_to_all x1 -> x0, starting transfers between devices: 7.44 us -> none  [body(): lax.all_to_all(outgoing, 'tile', split_axis=0, concat_axis=0, tiled=True)]
    select_n x5 -> x0, other arithmetic: 5.29 us -> none  [the longest x2 4.59 us: body(): outgoing = jnp.take(owned_blocks[0], send_slots, axis=0)]
  transfers between devices with their start and end apart: 3 -> 9, of which waited for: 3 -> 3; matrix products, arithmetic and copies ran while one was open for 2% -> 1% of each run, Pallas kernels for 0% -> 0%
where the time goes in v1:
time: 92.9 us; the launch traced here: 92 us
  starting transfers between devices  59.1 us (64%)
  Pallas kernels  23.8 us (26%)
  waiting for transfers between devices  4.9 us (5%)
  local copies, waits for them, and re-layouts  1.61 us (2%)
  other arithmetic  1.33 us (1%)
  between operations  1.25 us (1%)
    ppermute x7, starting transfers between devices, body(): arrived.append(lax.ppermute(sent[r], 'tile', route))  56.9 us
    pallas_call x1, Pallas kernels, march(): pl.pallas_call(functools.partial(march_kernel, step_size, tile_count, til...  21.3 us
    ppermute x2, waiting for transfers between devices, swapped(): return lax.ppermute(block, axis, [(i, i ^ 1 << bit) for i in range(count)])  3.72 us
    pallas_call x1, Pallas kernels, gather(): pl.pallas_call(functools.partial(gather_kernel, tile_count, capacity), in...  2.55 us
    ppermute x2, starting transfers between devices, swapped(): return lax.ppermute(block, axis, [(i, i ^ 1 << bit) for i in range(count)])  2.18 us
  transfers between devices with their start and end apart: 9, of which 3 were waited for; matrix products, arithmetic and copies ran while one was open for 1% of the time, Pallas kernels for 0%

profile of v1, /device:TPU:0, one launch (start us, length us, event | category | flops | bytes accessed | tf_op | source)
XLA Modules:
  0.0 92.0 jit_solution(16925324540700982739)
XLA Ops:
  0.0 0.0 copy-start.7
  0.0 21.3 %march.1 = (s16[8,4,8,128]{3,2,1,0:T(8,128)(2,1)}, s16[8,4,8,128]{3,2,1,0:T(8,128)(2,1)}, s16[8,4,8,128]{3,2,1,0:T(8,128)(2,1)}, s16[8,4,8,128]{3,2,1,0:T(8,128)...) custom-call(s32[8]{0:T(128)} %bitcast.18, ...), custom_call_target="tpu_custom_call" | custom-call | tf_op jit(solution)/shard_map/march/pallas_call | solution.py:144
  21.3 25.3 %collective-permute-start = (s16[8,4,8,128]{3,2,1,0:T(8,128)(2,1)}, s16[8,4,8,128]{3,2,1,0:T(8,128)(2,1)S(1)}, u32[]{:S(2)}, u32[]{:S(2)}) collective-permute-start(s16[8,4,8,128]{3,2,1,0:T(8,128)(2,1)} %get-tuple-element.14), channel_id=1, source_target_pairs={{0,4},{4,8},{8,12},{12,16},{16,20},{20,24},{24,28},{28,0},{1,5},{5... | collective-permute-start | bytes 196616 | tf_op jit(solution)/shard_map/ppermute | solution.py:250
  46.6 23.9 %collective-permute-start.1 = (s16[8,4,8,128]{3,2,1,0:T(8,128)(2,1)}, s16[8,4,8,128]{3,2,1,0:T(8,128)(2,1)S(1)}, u32[]{:S(2)}, u32[]{:S(2)}) collective-permute-start(s16[8,4,8,128]{3,2,1,0:T(8,128)(2,1)} %get-tuple-element.15), channel_id=1, source_target_pairs={{0,8},{4,12},{8,16},{12,20},{16,24},{20,28},{24,0},{28,4},{1,9},{5... | collective-permute-start | bytes 196616 | tf_op jit(solution)/shard_map/ppermute | solution.py:250
  70.5 0.0 collective-permute-start.2
  70.5 0.0 collective-permute-start.3
  70.5 3.8 %collective-permute-start.4 = (s16[8,4,8,128]{3,2,1,0:T(8,128)(2,1)}, s16[8,4,8,128]{3,2,1,0:T(8,128)(2,1)S(1)}, u32[]{:S(2)}, u32[]{:S(2)}) collective-permute-start(s16[8,4,8,128]{3,2,1,0:T(8,128)(2,1)} %get-tuple-element.18), channel_id=1, source_target_pairs={{0,20},{4,24},{8,28},{12,0},{16,4},{20,8},{24,12},{28,16},{1,21},{... | collective-permute-start | bytes 196616 | tf_op jit(solution)/shard_map/ppermute | solution.py:250
  74.3 0.0 collective-permute-done.refs_5_
  74.4 0.0 copy-start
  74.4 2.4 %collective-permute-start.5 = (s16[8,4,8,128]{3,2,1,0:T(8,128)(2,1)}, s16[8,4,8,128]{3,2,1,0:T(8,128)(2,1)S(1)}, u32[]{:S(2)}, u32[]{:S(2)}) collective-permute-start(s16[8,4,8,128]{3,2,1,0:T(8,128)(2,1)} %get-tuple-element.19), channel_id=1, source_target_pairs={{0,24},{4,28},{8,0},{12,4},{16,8},{20,12},{24,16},{28,20},{1,25},{... | collective-permute-start | bytes 196616 | tf_op jit(solution)/shard_map/ppermute | solution.py:250
  76.7 0.0 collective-permute-done.1.refs_6_
  76.7 0.0 copy-start.1
  76.7 1.5 %collective-permute-start.6 = (s16[8,4,8,128]{3,2,1,0:T(8,128)(2,1)}, s16[8,4,8,128]{3,2,1,0:T(8,128)(2,1)S(1)}, u32[]{:S(2)}, u32[]{:S(2)}) collective-permute-start(s16[8,4,8,128]{3,2,1,0:T(8,128)(2,1)} %get-tuple-element.20), channel_id=1, source_target_pairs={{0,28},{4,0},{8,4},{12,8},{16,12},{20,16},{24,20},{28,24},{1,29},{... | collective-permute-start | bytes 196616 | tf_op jit(solution)/shard_map/ppermute | solution.py:250
  78.2 0.0 copy-done.7
  78.3 0.6 fusion.4
  80.0 0.0 collective-permute-done.2.refs_7_
  80.0 0.0 copy-start.2
  80.0 0.0 collective-permute-done.3.refs_8_
  80.0 0.0 copy-start.3
  80.0 0.0 collective-permute-done.4.refs_9_
  80.0 0.0 copy-start.4
  80.0 0.0 collective-permute-done.5.refs_10_
  80.0 0.0 copy-start.5
  80.0 1.2 %collective-permute-done.6.refs_11_ = s16[8,4,8,128]{3,2,1,0:T(8,128)(2,1)S(1)} collective-permute-done((s16[8,4,8,128]{3,2,1,0:T(8,128)(2,1)}, s16[8,4,8,128]{3,2,1,0:T(8,128)(2,1)S(1)}, u32[]{:S(2)}, u32[]{:S(2)}) %collective-permute-start.6) | collective-permute-done | bytes 65568 | tf_op jit(solution)/shard_map/ppermute | solution.py:250
  81.2 0.0 copy-start.6
  81.2 0.0 copy-done
  81.2 0.0 copy-done.1
  81.2 0.0 copy-done.2
  81.2 0.0 copy-done.3
  81.2 0.0 copy-done.4
  81.2 0.0 copy-done.5
  81.2 0.6 copy-done.6
  81.8 2.6 %gather.1 = f32[4,128,128]{2,1,0:T(8,128)} custom-call(s32[8]{0:T(128)} %bitcast.19, s32[8]{0:T(128)} %bitcast.21, s32[8]{0:T(128)} %refs_2_.3, s32[1]{0:T(128)} %bitcast.2.refs_3_, s16[8,4,8,128]{3,2,1,0:T(8,128)(2,1)} %get-tuple-element.13.refs_4_, s16[8,4,8,128]{3,2,1,0:T(8,128)(2,1)} %copy-done, s16[8,4,8,128]{3,2,1,0:T(8,128)(2,1)} %copy-done.1, ...), custom_call_target="tpu_custom_call" | custom-call | tf_op jit(solution)/shard_map/gather/pallas_call | solution.py:219
  84.4 1.0 %fusion.5 = (f32[4,2,1,32,128]{4,3,2,1,0:T(8,128)S(1)}, f32[4,2,1,32,128]{4,3,2,1,0:T(8,128)S(1)}) fusion(f32[4,2,2,32,128]{4,3,2,1,0:T(8,128)} %bitcast.17), kind=kLoop, calls=%fused_computation.16 | loop fusion | bytes 524288 | tf_op jit(solution)/shard_map/slice | solution.py:260
  85.4 0.1 collective-permute-start.7
  85.5 1.3 %collective-permute-done.7 = f32[4,2,1,32,128]{4,3,0,2,1:T(8,128)S(1)} collective-permute-done((f32[4,2,1,32,128]{4,3,0,2,1:T(8,128)S(1)}, f32[4,2,1,32,128]{4,3,0,2,1:T(8,128)S(1)}, u32[]{:S(2)}, u32[]{:S(2)}) %collective-permute-start.7) | collective-permute-done | bytes 131104 | tf_op jit(solution)/shard_map/ppermute | solution.py:236
  86.9 2.1 %collective-permute-start.8 = (f32[4,1,1,32,128]{4,3,0,2,1:T(8,128)S(1)}, f32[4,1,1,32,128]{4,3,0,2,1:T(8,128)S(1)}, u32[]{:S(2)}, u32[]{:S(2)}) collective-permute-start(f32[4,1,1,32,128]{4,3,0,2,1:T(8,128)S(1)} %get-tuple-element.26), channel_id=1, source_target_pairs={{0,2},{1,3},{2,0},{3,1},{4,6},{5,7},{6,4},{7,5},{8,10},{9,11},{10,... | collective-permute-start | bytes 196616 | tf_op jit(solution)/shard_map/ppermute | solution.py:236
  89.0 2.4 %collective-permute-done.8 = f32[4,1,1,32,128]{4,3,0,2,1:T(8,128)S(1)} collective-permute-done((f32[4,1,1,32,128]{4,3,0,2,1:T(8,128)S(1)}, f32[4,1,1,32,128]{4,3,0,2,1:T(8,128)S(1)}, u32[]{:S(2)}, u32[]{:S(2)}) %collective-permute-start.8) | collective-permute-done | bytes 65568 | tf_op jit(solution)/shard_map/ppermute | solution.py:236
  91.4 0.6 select_bitcast_fusion
  (7 shorter events, 0.1 us)
Async XLA Ops:
  0.0 78.2 %copy-start.7 = (s32[8]{0:T(128)S(1)}, s32[8]{0:T(128)}, u32[]{:S(2)}) copy-start(s32[8]{0:T(128)} %refs_2_.3) | copy-start | bytes 100
  21.3 53.1 %collective-permute-start = (s16[8,4,8,128]{3,2,1,0:T(8,128)(2,1)}, s16[8,4,8,128]{3,2,1,0:T(8,128)(2,1)S(1)}, u32[]{:S(2)}, u32[]{:S(2)}) collective-permute-start(s16[8,4,8,128]{3,2,1,0:T(8,128)(2,1)} %get-tuple-element.14), channel_id=1, source_target_pairs={{0,4},{4,8},{8,12},{12,16},{16,20},{20,24},{24,28},{28,0},{1,5},{5... | collective-permute-start | bytes 196616 | tf_op jit(solution)/shard_map/ppermute | solution.py:250
  46.6 30.1 %collective-permute-start.1 = (s16[8,4,8,128]{3,2,1,0:T(8,128)(2,1)}, s16[8,4,8,128]{3,2,1,0:T(8,128)(2,1)S(1)}, u32[]{:S(2)}, u32[]{:S(2)}) collective-permute-start(s16[8,4,8,128]{3,2,1,0:T(8,128)(2,1)} %get-tuple-element.15), channel_id=1, source_target_pairs={{0,8},{4,12},{8,16},{12,20},{16,24},{20,28},{24,0},{28,4},{1,9},{5... | collective-permute-start | bytes 196616 | tf_op jit(solution)/shard_map/ppermute | solution.py:250
  70.5 9.4 %collective-permute-start.2 = (s16[8,4,8,128]{3,2,1,0:T(8,128)(2,1)}, s16[8,4,8,128]{3,2,1,0:T(8,128)(2,1)S(1)}, u32[]{:S(2)}, u32[]{:S(2)}) collective-permute-start(s16[8,4,8,128]{3,2,1,0:T(8,128)(2,1)} %get-tuple-element.16), channel_id=1, source_target_pairs={{0,12},{4,16},{8,20},{12,24},{16,28},{20,0},{24,4},{28,8},{1,13},{... | collective-permute-start | bytes 196616 | tf_op jit(solution)/shard_map/ppermute | solution.py:250
  70.5 9.5 %collective-permute-start.3 = (s16[8,4,8,128]{3,2,1,0:T(8,128)(2,1)}, s16[8,4,8,128]{3,2,1,0:T(8,128)(2,1)S(1)}, u32[]{:S(2)}, u32[]{:S(2)}) collective-permute-start(s16[8,4,8,128]{3,2,1,0:T(8,128)(2,1)} %get-tuple-element.17), channel_id=1, source_target_pairs={{0,16},{4,20},{8,24},{12,28},{16,0},{20,4},{24,8},{28,12},{1,17},{... | collective-permute-start | bytes 196616 | tf_op jit(solution)/shard_map/ppermute | solution.py:250
  70.5 9.5 %collective-permute-start.4 = (s16[8,4,8,128]{3,2,1,0:T(8,128)(2,1)}, s16[8,4,8,128]{3,2,1,0:T(8,128)(2,1)S(1)}, u32[]{:S(2)}, u32[]{:S(2)}) collective-permute-start(s16[8,4,8,128]{3,2,1,0:T(8,128)(2,1)} %get-tuple-element.18), channel_id=1, source_target_pairs={{0,20},{4,24},{8,28},{12,0},{16,4},{20,8},{24,12},{28,16},{1,21},{... | collective-permute-start | bytes 196616 | tf_op jit(solution)/shard_map/ppermute | solution.py:250
  74.4 6.9 %copy-start = (s16[8,4,8,128]{3,2,1,0:T(8,128)(2,1)}, s16[8,4,8,128]{3,2,1,0:T(8,128)(2,1)S(1)}, u32[]{:S(2)}) copy-start(s16[8,4,8,128]{3,2,1,0:T(8,128)(2,1)S(1)} %collective-permute-done.refs_5_) | copy-start | bytes 196612
  74.4 5.7 %collective-permute-start.5 = (s16[8,4,8,128]{3,2,1,0:T(8,128)(2,1)}, s16[8,4,8,128]{3,2,1,0:T(8,128)(2,1)S(1)}, u32[]{:S(2)}, u32[]{:S(2)}) collective-permute-start(s16[8,4,8,128]{3,2,1,0:T(8,128)(2,1)} %get-tuple-element.19), channel_id=1, source_target_pairs={{0,24},{4,28},{8,0},{12,4},{16,8},{20,12},{24,16},{28,20},{1,25},{... | collective-permute-start | bytes 196616 | tf_op jit(solution)/shard_map/ppermute | solution.py:250
  76.7 4.5 %copy-start.1 = (s16[8,4,8,128]{3,2,1,0:T(8,128)(2,1)}, s16[8,4,8,128]{3,2,1,0:T(8,128)(2,1)S(1)}, u32[]{:S(2)}) copy-start(s16[8,4,8,128]{3,2,1,0:T(8,128)(2,1)S(1)} %collective-permute-done.1.refs_6_) | copy-start | bytes 196612
  76.7 4.5 %collective-permute-start.6 = (s16[8,4,8,128]{3,2,1,0:T(8,128)(2,1)}, s16[8,4,8,128]{3,2,1,0:T(8,128)(2,1)S(1)}, u32[]{:S(2)}, u32[]{:S(2)}) collective-permute-start(s16[8,4,8,128]{3,2,1,0:T(8,128)(2,1)} %get-tuple-element.20), channel_id=1, source_target_pairs={{0,28},{4,0},{8,4},{12,8},{16,12},{20,16},{24,20},{28,24},{1,29},{... | collective-permute-start | bytes 196616 | tf_op jit(solution)/shard_map/ppermute | solution.py:250
  80.0 1.2 %copy-start.2 = (s16[8,4,8,128]{3,2,1,0:T(8,128)(2,1)}, s16[8,4,8,128]{3,2,1,0:T(8,128)(2,1)S(1)}, u32[]{:S(2)}) copy-start(s16[8,4,8,128]{3,2,1,0:T(8,128)(2,1)S(1)} %collective-permute-done.2.refs_7_) | copy-start | bytes 196612
  80.0 1.2 %copy-start.3 = (s16[8,4,8,128]{3,2,1,0:T(8,128)(2,1)}, s16[8,4,8,128]{3,2,1,0:T(8,128)(2,1)S(1)}, u32[]{:S(2)}) copy-start(s16[8,4,8,128]{3,2,1,0:T(8,128)(2,1)S(1)} %collective-permute-done.3.refs_8_) | copy-start | bytes 196612
  80.0 1.2 %copy-start.4 = (s16[8,4,8,128]{3,2,1,0:T(8,128)(2,1)}, s16[8,4,8,128]{3,2,1,0:T(8,128)(2,1)S(1)}, u32[]{:S(2)}) copy-start(s16[8,4,8,128]{3,2,1,0:T(8,128)(2,1)S(1)} %collective-permute-done.4.refs_9_) | copy-start | bytes 196612
  80.0 1.2 %copy-start.5 = (s16[8,4,8,128]{3,2,1,0:T(8,128)(2,1)}, s16[8,4,8,128]{3,2,1,0:T(8,128)(2,1)S(1)}, u32[]{:S(2)}) copy-start(s16[8,4,8,128]{3,2,1,0:T(8,128)(2,1)S(1)} %collective-permute-done.5.refs_10_) | copy-start | bytes 196612
  81.2 0.6 copy-start.6
  85.4 1.4 %collective-permute-start.7 = (f32[4,2,1,32,128]{4,3,0,2,1:T(8,128)S(1)}, f32[4,2,1,32,128]{4,3,0,2,1:T(8,128)S(1)}, u32[]{:S(2)}, u32[]{:S(2)}) collective-permute-start(f32[4,2,1,32,128]{4,3,0,2,1:T(8,128)S(1)} %get-tuple-element.22), channel_id=1, source_target_pairs={{0,1},{1,0},{2,3},{3,2},{4,5},{5,4},{6,7},{7,6},{8,9},{9,8},{10,11... | collective-permute-start | bytes 393224 | tf_op jit(solution)/shard_map/ppermute | solution.py:236
  86.9 4.5 %collective-permute-start.8 = (f32[4,1,1,32,128]{4,3,0,2,1:T(8,128)S(1)}, f32[4,1,1,32,128]{4,3,0,2,1:T(8,128)S(1)}, u32[]{:S(2)}, u32[]{:S(2)}) collective-permute-start(f32[4,1,1,32,128]{4,3,0,2,1:T(8,128)S(1)} %get-tuple-element.26), channel_id=1, source_target_pairs={{0,2},{1,3},{2,0},{3,1},{4,6},{5,7},{6,4},{7,5},{8,10},{9,11},{10,... | collective-permute-start | bytes 196616 | tf_op jit(solution)/shard_map/ppermute | solution.py:236

commit v2 on v1

--- a/solution.py
+++ b/solution.py
@@ -22,6 +22,7 @@
 CODE_TOP = 65535.0
 CODE_MID = 32767.5
 WIDE = 2
+UNROLL = 16
 
 
 def exclusive_start(counts_ref, index, tile_count):
@@ -39,7 +40,7 @@
 
 
 def encode(image):
-    root = jnp.sqrt(jnp.sqrt(jnp.maximum(image, 0.0)))
+    root = jnp.exp2(jnp.log(jnp.maximum(image, 0.0)) * (0.25 * LOG2E))
     code = jnp.round(jnp.minimum(root, 1.0) * CODE_TOP - CODE_MID)
     return code.astype(jnp.int32).astype(jnp.int16)
 
@@ -113,7 +114,7 @@
 
                 zero = jnp.zeros((8, LANES), jnp.float32)
                 first = tuple((zero, zero + 1.0, zero, zero, zero) for j in range(WIDE))
-                last = lax.fori_loop(0, BLOCK, depth, first)
+                last = lax.fori_loop(0, BLOCK, depth, first, unroll=UNROLL)
                 for j in range(WIDE):
                     total, seen, reds, greens, blues = last[j]
                     passed = jnp.exp2(total * (-step_size * LOG2E))

time: 92.9 us -> 61.2 us (0.66)
  starting transfers between devices: 59.1 us -> 20.7 us
  Pallas kernels: 23.8 us -> 29.2 us
  waiting for transfers between devices: 4.9 us -> 6.79 us
    ppermute x7, starting transfers between devices: 56.9 us -> 19.1 us  [body(): arrived.append(lax.ppermute(sent[r], 'tile', route))]
    pallas_call x1, Pallas kernels: 21.3 us -> 26.6 us  [march(): pl.pallas_call(functools.partial(march_kernel, step_size, tile_count, til...]
    ppermute x7, waiting for transfers between devices: 1.18 us -> 2.7 us  [body(): arrived.append(lax.ppermute(sent[r], 'tile', route))]
  transfers between devices with their start and end apart: 9 -> 9, of which waited for: 3 -> 4; matrix products, arithmetic and copies ran while one was open for 1% -> 1% of each run, Pallas kernels for 0% -> 0%
where the time goes in v2:
time: 61.2 us; the launch traced here: 60.9 us
  Pallas kernels  29.2 us (48%)
  starting transfers between devices  20.7 us (34%)
  waiting for transfers between devices  6.79 us (11%)
  local copies, waits for them, and re-layouts  1.61 us (3%)
  other arithmetic  1.33 us (2%)
  between operations  1.26 us (2%)
    pallas_call x1, Pallas kernels, march(): pl.pallas_call(functools.partial(march_kernel, step_size, tile_count, til...  26.6 us
    ppermute x7, starting transfers between devices, body(): arrived.append(lax.ppermute(sent[r], 'tile', route))  19.1 us
    ppermute x2, waiting for transfers between devices, swapped(): return lax.ppermute(block, axis, [(i, i ^ 1 << bit) for i in range(count)])  4.09 us
    ppermute x7, waiting for transfers between devices, body(): arrived.append(lax.ppermute(sent[r], 'tile', route))  2.7 us
    pallas_call x1, Pallas kernels, gather(): pl.pallas_call(functools.partial(gather_kernel, tile_count, capacity), in...  2.55 us
    ppermute x2, starting transfers between devices, swapped(): return lax.ppermute(block, axis, [(i, i ^ 1 << bit) for i in range(count)])  1.63 us
  transfers between devices with their start and end apart: 9, of which 4 were waited for; matrix products, arithmetic and copies ran while one was open for 1% of the time, Pallas kernels for 0%

profile of v2, /device:TPU:0, one launch (start us, length us, event | category | flops | bytes accessed | tf_op | source)
XLA Modules:
  0.0 60.9 jit_solution(15344270571063423336)
XLA Ops:
  0.0 0.0 copy-start.7
  0.0 26.6 %march.1 = (s16[8,4,8,128]{3,2,1,0:T(8,128)(2,1)}, s16[8,4,8,128]{3,2,1,0:T(8,128)(2,1)}, s16[8,4,8,128]{3,2,1,0:T(8,128)(2,1)}, s16[8,4,8,128]{3,2,1,0:T(8,128)...) custom-call(s32[8]{0:T(128)} %bitcast.18, ...), custom_call_target="tpu_custom_call" | custom-call | tf_op jit(solution)/shard_map/march/pallas_call | solution.py:145
  26.6 0.1 collective-permute-start
  26.7 0.1 collective-permute-start.1
  26.8 12.3 %collective-permute-start.2 = (s16[8,4,8,128]{3,2,1,0:T(8,128)(2,1)}, s16[8,4,8,128]{3,2,1,0:T(8,128)(2,1)S(1)}, u32[]{:S(2)}, u32[]{:S(2)}) collective-permute-start(s16[8,4,8,128]{3,2,1,0:T(8,128)(2,1)} %get-tuple-element.16), channel_id=1, source_target_pairs={{0,12},{4,16},{8,20},{12,24},{16,28},{20,0},{24,4},{28,8},{1,13},{... | collective-permute-start | bytes 196616 | tf_op jit(solution)/shard_map/ppermute | solution.py:251
  39.1 0.0 collective-permute-start.3
  39.1 3.8 %collective-permute-start.4 = (s16[8,4,8,128]{3,2,1,0:T(8,128)(2,1)}, s16[8,4,8,128]{3,2,1,0:T(8,128)(2,1)S(1)}, u32[]{:S(2)}, u32[]{:S(2)}) collective-permute-start(s16[8,4,8,128]{3,2,1,0:T(8,128)(2,1)} %get-tuple-element.18), channel_id=1, source_target_pairs={{0,20},{4,24},{8,28},{12,0},{16,4},{20,8},{24,12},{28,16},{1,21},{... | collective-permute-start | bytes 196616 | tf_op jit(solution)/shard_map/ppermute | solution.py:251
  42.8 0.0 collective-permute-done.refs_5_
  42.8 0.0 copy-start
  42.9 2.9 %collective-permute-start.5 = (s16[8,4,8,128]{3,2,1,0:T(8,128)(2,1)}, s16[8,4,8,128]{3,2,1,0:T(8,128)(2,1)S(1)}, u32[]{:S(2)}, u32[]{:S(2)}) collective-permute-start(s16[8,4,8,128]{3,2,1,0:T(8,128)(2,1)} %get-tuple-element.19), channel_id=1, source_target_pairs={{0,24},{4,28},{8,0},{12,4},{16,8},{20,12},{24,16},{28,20},{1,25},{... | collective-permute-start | bytes 196616 | tf_op jit(solution)/shard_map/ppermute | solution.py:251
  45.8 0.0 collective-permute-done.1.refs_6_
  45.8 0.0 copy-start.1
  45.8 0.0 collective-permute-start.6
  45.8 0.0 copy-done.7
  45.8 0.6 fusion.4
  47.5 0.0 collective-permute-done.2.refs_7_
  47.5 0.0 copy-start.2
  47.5 0.0 collective-permute-done.3.refs_8_
  47.5 0.0 copy-start.3
  47.5 0.0 collective-permute-done.4.refs_9_
  47.6 0.0 copy-start.4
  47.6 1.7 %collective-permute-done.5.refs_10_ = s16[8,4,8,128]{3,2,1,0:T(8,128)(2,1)S(1)} collective-permute-done((s16[8,4,8,128]{3,2,1,0:T(8,128)(2,1)}, s16[8,4,8,128]{3,2,1,0:T(8,128)(2,1)S(1)}, u32[]{:S(2)}, u32[]{:S(2)}) %collective-permute-start.5) | collective-permute-done | bytes 65568 | tf_op jit(solution)/shard_map/ppermute | solution.py:251
  49.3 0.0 copy-start.5
  49.3 1.0 %collective-permute-done.6.refs_11_ = s16[8,4,8,128]{3,2,1,0:T(8,128)(2,1)S(1)} collective-permute-done((s16[8,4,8,128]{3,2,1,0:T(8,128)(2,1)}, s16[8,4,8,128]{3,2,1,0:T(8,128)(2,1)S(1)}, u32[]{:S(2)}, u32[]{:S(2)}) %collective-permute-start.6) | collective-permute-done | bytes 65568 | tf_op jit(solution)/shard_map/ppermute | solution.py:251
  50.3 0.0 copy-start.6
  50.3 0.0 copy-done
  50.3 0.0 copy-done.1
  50.3 0.0 copy-done.2
  50.3 0.0 copy-done.3
  50.3 0.0 copy-done.4
  50.3 0.0 copy-done.5
  50.3 0.6 copy-done.6
  50.9 2.6 %gather.1 = f32[4,128,128]{2,1,0:T(8,128)} custom-call(s32[8]{0:T(128)} %bitcast.19, s32[8]{0:T(128)} %bitcast.21, s32[8]{0:T(128)} %refs_2_.3, s32[1]{0:T(128)} %bitcast.2.refs_3_, s16[8,4,8,128]{3,2,1,0:T(8,128)(2,1)} %get-tuple-element.13.refs_4_, s16[8,4,8,128]{3,2,1,0:T(8,128)(2,1)} %copy-done, s16[8,4,8,128]{3,2,1,0:T(8,128)(2,1)} %copy-done.1, ...), custom_call_target="tpu_custom_call" | custom-call | tf_op jit(solution)/shard_map/gather/pallas_call | solution.py:220
  53.4 1.0 %fusion.5 = (f32[4,2,1,32,128]{4,3,2,1,0:T(8,128)S(1)}, f32[4,2,1,32,128]{4,3,2,1,0:T(8,128)S(1)}) fusion(f32[4,2,2,32,128]{4,3,2,1,0:T(8,128)} %bitcast.17), kind=kLoop, calls=%fused_computation.16 | loop fusion | bytes 524288 | tf_op jit(solution)/shard_map/slice | solution.py:261
  54.5 0.1 collective-permute-start.7
  54.6 1.3 %collective-permute-done.7 = f32[4,2,1,32,128]{4,3,0,2,1:T(8,128)S(1)} collective-permute-done((f32[4,2,1,32,128]{4,3,0,2,1:T(8,128)S(1)}, f32[4,2,1,32,128]{4,3,0,2,1:T(8,128)S(1)}, u32[]{:S(2)}, u32[]{:S(2)}) %collective-permute-start.7) | collective-permute-done | bytes 131104 | tf_op jit(solution)/shard_map/ppermute | solution.py:237
  55.9 1.6 %collective-permute-start.8 = (f32[4,1,1,32,128]{4,3,0,2,1:T(8,128)S(1)}, f32[4,1,1,32,128]{4,3,0,2,1:T(8,128)S(1)}, u32[]{:S(2)}, u32[]{:S(2)}) collective-permute-start(f32[4,1,1,32,128]{4,3,0,2,1:T(8,128)S(1)} %get-tuple-element.26), channel_id=1, source_target_pairs={{0,2},{1,3},{2,0},{3,1},{4,6},{5,7},{6,4},{7,5},{8,10},{9,11},{10,... | collective-permute-start | bytes 196616 | tf_op jit(solution)/shard_map/ppermute | solution.py:237
  57.5 2.8 %collective-permute-done.8 = f32[4,1,1,32,128]{4,3,0,2,1:T(8,128)S(1)} collective-permute-done((f32[4,1,1,32,128]{4,3,0,2,1:T(8,128)S(1)}, f32[4,1,1,32,128]{4,3,0,2,1:T(8,128)S(1)}, u32[]{:S(2)}, u32[]{:S(2)}) %collective-permute-start.8) | collective-permute-done | bytes 65568 | tf_op jit(solution)/shard_map/ppermute | solution.py:237
  60.3 0.6 %select_bitcast_fusion = f32[4,32,128]{2,1,0:T(8,128)} fusion(f32[4,1,1,32,128]{4,3,0,2,1:T(8,128)S(1)} %collective-permute-done.8, f32[4,1,1,32,128]{4,3,0,2,1:T(8,128)S(1)} %get-tuple-element.25, f32[32,128]{1,0:T(8,128)S(1)} %fusion.2, f32[32,128]{1,0:T(8,128)S(1)} %fusion.3, pred[]{:T(512)S(6)} %eq.22), kind=kLoop, calls=%fused_computation.3 | loop fusion | flops 81920 | bytes 229377 | tf_op jit(solution)/shard_map/reshape | solution.py:270
  (7 shorter events, 0.1 us)
Async XLA Ops:
  0.0 45.8 %copy-start.7 = (s32[8]{0:T(128)S(1)}, s32[8]{0:T(128)}, u32[]{:S(2)}) copy-start(s32[8]{0:T(128)} %refs_2_.3) | copy-start | bytes 100
  26.6 16.2 %collective-permute-start = (s16[8,4,8,128]{3,2,1,0:T(8,128)(2,1)}, s16[8,4,8,128]{3,2,1,0:T(8,128)(2,1)S(1)}, u32[]{:S(2)}, u32[]{:S(2)}) collective-permute-start(s16[8,4,8,128]{3,2,1,0:T(8,128)(2,1)} %get-tuple-element.14), channel_id=1, source_target_pairs={{0,4},{4,8},{8,12},{12,16},{16,20},{20,24},{24,28},{28,0},{1,5},{5... | collective-permute-start | bytes 196616 | tf_op jit(solution)/shard_map/ppermute | solution.py:251
  26.7 19.1 %collective-permute-start.1 = (s16[8,4,8,128]{3,2,1,0:T(8,128)(2,1)}, s16[8,4,8,128]{3,2,1,0:T(8,128)(2,1)S(1)}, u32[]{:S(2)}, u32[]{:S(2)}) collective-permute-start(s16[8,4,8,128]{3,2,1,0:T(8,128)(2,1)} %get-tuple-element.15), channel_id=1, source_target_pairs={{0,8},{4,12},{8,16},{12,20},{16,24},{20,28},{24,0},{28,4},{1,9},{5... | collective-permute-start | bytes 196616 | tf_op jit(solution)/shard_map/ppermute | solution.py:251
  26.8 20.7 %collective-permute-start.2 = (s16[8,4,8,128]{3,2,1,0:T(8,128)(2,1)}, s16[8,4,8,128]{3,2,1,0:T(8,128)(2,1)S(1)}, u32[]{:S(2)}, u32[]{:S(2)}) collective-permute-start(s16[8,4,8,128]{3,2,1,0:T(8,128)(2,1)} %get-tuple-element.16), channel_id=1, source_target_pairs={{0,12},{4,16},{8,20},{12,24},{16,28},{20,0},{24,4},{28,8},{1,13},{... | collective-permute-start | bytes 196616 | tf_op jit(solution)/shard_map/ppermute | solution.py:251
  39.1 8.4 %collective-permute-start.3 = (s16[8,4,8,128]{3,2,1,0:T(8,128)(2,1)}, s16[8,4,8,128]{3,2,1,0:T(8,128)(2,1)S(1)}, u32[]{:S(2)}, u32[]{:S(2)}) collective-permute-start(s16[8,4,8,128]{3,2,1,0:T(8,128)(2,1)} %get-tuple-element.17), channel_id=1, source_target_pairs={{0,16},{4,20},{8,24},{12,28},{16,0},{20,4},{24,8},{28,12},{1,17},{... | collective-permute-start | bytes 196616 | tf_op jit(solution)/shard_map/ppermute | solution.py:251
  39.1 8.5 %collective-permute-start.4 = (s16[8,4,8,128]{3,2,1,0:T(8,128)(2,1)}, s16[8,4,8,128]{3,2,1,0:T(8,128)(2,1)S(1)}, u32[]{:S(2)}, u32[]{:S(2)}) collective-permute-start(s16[8,4,8,128]{3,2,1,0:T(8,128)(2,1)} %get-tuple-element.18), channel_id=1, source_target_pairs={{0,20},{4,24},{8,28},{12,0},{16,4},{20,8},{24,12},{28,16},{1,21},{... | collective-permute-start | bytes 196616 | tf_op jit(solution)/shard_map/ppermute | solution.py:251
  42.8 7.4 %copy-start = (s16[8,4,8,128]{3,2,1,0:T(8,128)(2,1)}, s16[8,4,8,128]{3,2,1,0:T(8,128)(2,1)S(1)}, u32[]{:S(2)}) copy-start(s16[8,4,8,128]{3,2,1,0:T(8,128)(2,1)S(1)} %collective-permute-done.refs_5_) | copy-start | bytes 196612
  42.9 6.4 %collective-permute-start.5 = (s16[8,4,8,128]{3,2,1,0:T(8,128)(2,1)}, s16[8,4,8,128]{3,2,1,0:T(8,128)(2,1)S(1)}, u32[]{:S(2)}, u32[]{:S(2)}) collective-permute-start(s16[8,4,8,128]{3,2,1,0:T(8,128)(2,1)} %get-tuple-element.19), channel_id=1, source_target_pairs={{0,24},{4,28},{8,0},{12,4},{16,8},{20,12},{24,16},{28,20},{1,25},{... | collective-permute-start | bytes 196616 | tf_op jit(solution)/shard_map/ppermute | solution.py:251
  45.8 4.5 %copy-start.1 = (s16[8,4,8,128]{3,2,1,0:T(8,128)(2,1)}, s16[8,4,8,128]{3,2,1,0:T(8,128)(2,1)S(1)}, u32[]{:S(2)}) copy-start(s16[8,4,8,128]{3,2,1,0:T(8,128)(2,1)S(1)} %collective-permute-done.1.refs_6_) | copy-start | bytes 196612
  45.8 4.5 %collective-permute-start.6 = (s16[8,4,8,128]{3,2,1,0:T(8,128)(2,1)}, s16[8,4,8,128]{3,2,1,0:T(8,128)(2,1)S(1)}, u32[]{:S(2)}, u32[]{:S(2)}) collective-permute-start(s16[8,4,8,128]{3,2,1,0:T(8,128)(2,1)} %get-tuple-element.20), channel_id=1, source_target_pairs={{0,28},{4,0},{8,4},{12,8},{16,12},{20,16},{24,20},{28,24},{1,29},{... | collective-permute-start | bytes 196616 | tf_op jit(solution)/shard_map/ppermute | solution.py:251
  47.5 2.8 %copy-start.2 = (s16[8,4,8,128]{3,2,1,0:T(8,128)(2,1)}, s16[8,4,8,128]{3,2,1,0:T(8,128)(2,1)S(1)}, u32[]{:S(2)}) copy-start(s16[8,4,8,128]{3,2,1,0:T(8,128)(2,1)S(1)} %collective-permute-done.2.refs_7_) | copy-start | bytes 196612
  47.5 2.7 %copy-start.3 = (s16[8,4,8,128]{3,2,1,0:T(8,128)(2,1)}, s16[8,4,8,128]{3,2,1,0:T(8,128)(2,1)S(1)}, u32[]{:S(2)}) copy-start(s16[8,4,8,128]{3,2,1,0:T(8,128)(2,1)S(1)} %collective-permute-done.3.refs_8_) | copy-start | bytes 196612
  47.6 2.7 %copy-start.4 = (s16[8,4,8,128]{3,2,1,0:T(8,128)(2,1)}, s16[8,4,8,128]{3,2,1,0:T(8,128)(2,1)S(1)}, u32[]{:S(2)}) copy-start(s16[8,4,8,128]{3,2,1,0:T(8,128)(2,1)S(1)} %collective-permute-done.4.refs_9_) | copy-start | bytes 196612
  49.3 1.0 %copy-start.5 = (s16[8,4,8,128]{3,2,1,0:T(8,128)(2,1)}, s16[8,4,8,128]{3,2,1,0:T(8,128)(2,1)S(1)}, u32[]{:S(2)}) copy-start(s16[8,4,8,128]{3,2,1,0:T(8,128)(2,1)S(1)} %collective-permute-done.5.refs_10_) | copy-start | bytes 196612
  50.3 0.6 %copy-start.6 = (s16[8,4,8,128]{3,2,1,0:T(8,128)(2,1)}, s16[8,4,8,128]{3,2,1,0:T(8,128)(2,1)S(1)}, u32[]{:S(2)}) copy-start(s16[8,4,8,128]{3,2,1,0:T(8,128)(2,1)S(1)} %collective-permute-done.6.refs_11_) | copy-start | bytes 196612
  54.5 1.4 %collective-permute-start.7 = (f32[4,2,1,32,128]{4,3,0,2,1:T(8,128)S(1)}, f32[4,2,1,32,128]{4,3,0,2,1:T(8,128)S(1)}, u32[]{:S(2)}, u32[]{:S(2)}) collective-permute-start(f32[4,2,1,32,128]{4,3,0,2,1:T(8,128)S(1)} %get-tuple-element.22), channel_id=1, source_target_pairs={{0,1},{1,0},{2,3},{3,2},{4,5},{5,4},{6,7},{7,6},{8,9},{9,8},{10,11... | collective-permute-start | bytes 393224 | tf_op jit(solution)/shard_map/ppermute | solution.py:237
  55.9 4.3 %collective-permute-start.8 = (f32[4,1,1,32,128]{4,3,0,2,1:T(8,128)S(1)}, f32[4,1,1,32,128]{4,3,0,2,1:T(8,128)S(1)}, u32[]{:S(2)}, u32[]{:S(2)}) collective-permute-start(f32[4,1,1,32,128]{4,3,0,2,1:T(8,128)S(1)} %get-tuple-element.26), channel_id=1, source_target_pairs={{0,2},{1,3},{2,0},{3,1},{4,6},{5,7},{6,4},{7,5},{8,10},{9,11},{10,... | collective-permute-start | bytes 196616 | tf_op jit(solution)/shard_map/ppermute | solution.py:237

commit v3 on v2

--- a/solution.py
+++ b/solution.py
@@ -21,6 +21,8 @@
 ROOT = math.sqrt(BUMP_SCALE * LOG2E)
 CODE_TOP = 65535.0
 CODE_MID = 32767.5
+GRANT = 12 << 20
+MARCH_GRANT = 61 << 20
 WIDE = 2
 UNROLL = 16
 
@@ -156,30 +158,40 @@
             pltpu.VMEM((KNOTS * 5, 8, LANES), jnp.float32),
             pltpu.VMEM((tile_count // 8, 4, 8 * TILES, LANES), jnp.float32),
         ],
+        compiler_params=pltpu.CompilerParams(vmem_limit_bytes=MARCH_GRANT),
         name="march",
     )(counts, order, flip, me, centers.reshape(1, KNOTS), amps, cells)
 
 
-def over(nearer, farther, uncovered):
-    return nearer + uncovered * farther
-
-
-def gather_kernel(tile_count, capacity, *refs):
+def split_rows(image, kept_ref, given_ref, low, row_share):
+    for n in range(kept_ref.shape[1] // row_share):
+        mine = pl.multiple_of((2 * n + low) * row_share, row_share)
+        theirs = pl.multiple_of((2 * n + 1 - low) * row_share, row_share)
+        for c in range(4):
+            kept_ref[c, n * row_share:(n + 1) * row_share] = image[c, pl.ds(mine, row_share)]
+            given_ref[c, n * row_share:(n + 1) * row_share] = image[c, pl.ds(theirs, row_share)]
+
+
+def gather_kernel(tile_count, row_share, *refs):
     counts_ref, order_ref, flip_ref, me_ref = refs[:4]
     arrived = refs[4:4 + tile_count]
-    out_ref, brick_ref = refs[4 + tile_count:]
+    kept_ref, given_ref, brick_ref, image_ref = refs[4 + tile_count:]
     me = me_ref[0]
     position = position_of(order_ref, me, tile_count)
+    starts = [jnp.int32(0)]
+    for i in range(tile_count):
+        starts.append(starts[-1] + counts_ref[i])
     for r in range(tile_count):
         owner = lax.rem(me - r + tile_count, tile_count)
-        start = exclusive_start(counts_ref, owner, tile_count)
+        start = jnp.int32(0)
+        for i in range(tile_count):
+            start = jnp.where(owner == i, starts[i], start)
         offset = lax.rem(position - start + tile_count * 64, tile_count)
         level = (start + offset - position) // tile_count
         held = (counts_ref[owner] - offset + tile_count - 1) // tile_count
 
         def place(m, carry, r=r, level=level):
-            for c in range(4):
-                brick_ref[level + m, c] = decode(arrived[r][m, c])
+            brick_ref[level + m] = decode(arrived[r][m])
             return carry
 
         lax.fori_loop(0, held, place, 0)
@@ -209,27 +221,69 @@
                     if turn:
                         moved = pltpu.roll(moved, turn, 1)
                     line = moved if line is None else jnp.where(lane == bx, moved, line)
-                out_ref[c, pl.ds(by * BLOCK + s, TILES, stride=per_row), :] = line
-
-
-def gather(counts, order, flip, me, arrived):
+                image_ref[c, pl.ds(by * BLOCK + s, TILES, stride=per_row), :] = line
+    split_rows(image_ref, kept_ref, given_ref, me_ref[1] & 1, row_share)
+
+
+def gather(counts, order, flip, me, arrived, row_share):
     tile_count = counts.shape[0]
-    capacity = arrived[0].shape[0]
     scalar = pl.BlockSpec(memory_space=pltpu.SMEM)
     vmem = pl.BlockSpec(memory_space=pltpu.VMEM)
+    rows, width = BY * BLOCK, BX * BLOCK
+    half = jax.ShapeDtypeStruct((4, rows // 2, width), jnp.float32)
     return pl.pallas_call(
-        functools.partial(gather_kernel, tile_count, capacity),
+        functools.partial(gather_kernel, tile_count, row_share),
         in_specs=[scalar] * 4 + [vmem] * tile_count,
-        out_specs=vmem,
-        out_shape=jax.ShapeDtypeStruct((4, BY * BLOCK, BX * BLOCK), jnp.float32),
-        scratch_shapes=[pltpu.VMEM((DB * BY * BX, 4, TILES, LANES), jnp.float32)],
+        out_specs=[vmem] * 2,
+        out_shape=[half, half],
+        scratch_shapes=[
+            pltpu.VMEM((DB * BY * BX, 4, TILES, LANES), jnp.float32),
+            pltpu.VMEM((4, rows, width), jnp.float32),
+        ],
+        compiler_params=pltpu.CompilerParams(vmem_limit_bytes=GRANT),
         name="gather",
     )(counts, order, flip, me, *arrived)
 
 
-def over_blend(nearer, farther, chan_axis):
-    coverage = lax.slice_in_dim(nearer, 3, 4, axis=chan_axis)
-    return nearer + (1.0 - coverage) * farther
+def blend_kernel(bit, row_share, *refs):
+    flip_ref, me_ref, kept_ref, other_ref = refs[:4]
+    side = me_ref[1] >> bit & 1
+    front = side == flip_ref[me_ref[0]]
+    last = len(refs) == 5
+    out_ref = refs[-1]
+
+    def blend(near_ref, far_ref):
+        uncovered = 1.0 - near_ref[3]
+        for c in range(4):
+            out_ref[c] = near_ref[c] + uncovered * far_ref[c]
+
+    @pl.when(front)
+    def _():
+        blend(kept_ref, other_ref)
+
+    @pl.when(jnp.logical_not(front))
+    def _():
+        blend(other_ref, kept_ref)
+
+    if not last:
+        split_rows(out_ref, refs[4], refs[5], me_ref[1] >> (bit + 1) & 1, row_share)
+
+
+def blend(flip, me, kept, other, bit, row_share):
+    scalar = pl.BlockSpec(memory_space=pltpu.SMEM)
+    vmem = pl.BlockSpec(memory_space=pltpu.VMEM)
+    last = kept.shape[1] == row_share
+    whole = jax.ShapeDtypeStruct(kept.shape, jnp.float32)
+    half = jax.ShapeDtypeStruct((4, kept.shape[1] // 2, kept.shape[2]), jnp.float32)
+    return pl.pallas_call(
+        functools.partial(blend_kernel, bit, row_share),
+        in_specs=[scalar] * 2 + [vmem] * 2,
+        out_specs=vmem if last else [vmem] * 2,
+        out_shape=whole if last else [half, half],
+        scratch_shapes=[] if last else [pltpu.VMEM(kept.shape, jnp.float32)],
+        compiler_params=pltpu.CompilerParams(vmem_limit_bytes=GRANT),
+        name="blend",
+    )(flip, me, kept, other)
 
 
 def swapped(block, axis, bit):
@@ -240,34 +294,23 @@
 def body(owned_blocks, slot_counts, brick_order, view_flip, tf_centers, tf_amps):
     tile_count = lax.axis_size("tile")
     depth_count = lax.axis_size("depth")
-    depth_index = lax.axis_index("depth")
     step_size = 1.5 / (depth_count * DB * BLOCK)
-    me = lax.axis_index("tile").astype(jnp.int32).reshape(1)
+    me = jnp.stack([lax.axis_index("tile"), lax.axis_index("depth")]).astype(jnp.int32)
     counts, order = slot_counts[0], brick_order[0]
     sent = march(counts, order, view_flip, me, tf_centers, tf_amps, owned_blocks[0], step_size)
     arrived = [sent[0]]
     for r in range(1, tile_count):
         route = [(i, (i + r) % tile_count) for i in range(tile_count)]
         arrived.append(lax.ppermute(sent[r], "tile", route))
-    tile_image = gather(counts, order, view_flip, me, arrived)
-    flip_mine = jnp.sum(jnp.where(jnp.arange(tile_count, dtype=jnp.int32) == me[0], view_flip, 0))
+    row_share = BY * BLOCK // depth_count
+    kept, given = gather(counts, order, view_flip, me, arrived, row_share)
     levels = depth_count.bit_length() - 1
-    row_share = tile_image.shape[1] // depth_count
-    width = tile_image.shape[2]
-    current = tile_image.reshape((4,) + (2,) * levels + (row_share, width))
-    for bit_index in range(levels):
-        split_axis = 1 + (levels - 1 - bit_index)
-        lower_half = lax.slice_in_dim(current, 0, 1, axis=split_axis)
-        upper_half = lax.slice_in_dim(current, 1, 2, axis=split_axis)
-        high_side = depth_index >> bit_index & 1
-        kept_half = jnp.where(high_side == 1, upper_half, lower_half)
-        given_half = jnp.where(high_side == 1, lower_half, upper_half)
-        other_half = swapped(given_half, "depth", bit_index)
-        mine_front = high_side == flip_mine
-        current = jnp.where(
-            mine_front, over_blend(kept_half, other_half, 0), over_blend(other_half, kept_half, 0)
-        )
-    return current.reshape(4, row_share, width)
+    for bit in range(levels):
+        other = swapped(given, "depth", bit)
+        blended = blend(view_flip, me, kept, other, bit, row_share)
+        if bit < levels - 1:
+            kept, given = blended
+    return blended
 
 
 def solution(mesh):

time: 61.2 us -> 59.7 us (0.975)
  starting transfers between devices: 20.7 us -> 37.6 us
  Pallas kernels: 29.2 us -> 12.9 us
  between operations: 1.26 us -> 0.07 us
  waiting for transfers between devices: 6.79 us -> 7.67 us
  local copies, waits for them, and re-layouts: 1.61 us -> 0.85 us
  other arithmetic: 1.33 us -> 0.59 us
    pallas_call x1, Pallas kernels: 26.6 us -> 9.78 us  [march(): pl.pallas_call(functools.partial(march_kernel, step_size, tile_count, til...]
    ppermute x7, starting transfers between devices: 19.1 us -> 35.8 us  [body(): arrived.append(lax.ppermute(sent[r], 'tile', route))]
    slice x1 -> x0, local copies, waits for them, and re-layouts: 0.99 us -> none  [body(): upper_half = lax.slice_in_dim(current, 1, 2, axis=split_axis)]
    ppermute x7, waiting for transfers between devices: 2.7 us -> 3.67 us  [body(): arrived.append(lax.ppermute(sent[r], 'tile', route))]
    reshape x1 -> x0, other arithmetic: 0.65 us -> none  [body(): return current.reshape(4, row_share, width)]
    pallas_call x1 -> x3, Pallas kernels: 2.55 us -> 3.14 us  [the longest x2 1.78 us: blend(): pl.pallas_call(functools.partial(blend_kernel, bit, row_share), in_specs=...]
  transfers between devices with their start and end apart: 9 -> 9, of which waited for: 4 -> 6; matrix products, arithmetic and copies ran while one was open for 1% -> 0% of each run, Pallas kernels for 0% -> 0%
where the time goes in v3:
time: 59.7 us; the launch traced here: 59.6 us
  starting transfers between devices  37.6 us (63%)
  Pallas kernels  12.9 us (22%)
  waiting for transfers between devices  7.67 us (13%)
  local copies, waits for them, and re-layouts  0.85 us (1%)
    ppermute x7, starting transfers between devices, body(): arrived.append(lax.ppermute(sent[r], 'tile', route))  35.8 us
    pallas_call x1, Pallas kernels, march(): pl.pallas_call(functools.partial(march_kernel, step_size, tile_count, til...  9.78 us
    ppermute x2, waiting for transfers between devices, swapped(): return lax.ppermute(block, axis, [(i, i ^ 1 << bit) for i in range(count)])  4.01 us
    ppermute x7, waiting for transfers between devices, body(): arrived.append(lax.ppermute(sent[r], 'tile', route))  3.67 us
    pallas_call x2, Pallas kernels, blend(): pl.pallas_call(functools.partial(blend_kernel, bit, row_share), in_specs=...  1.78 us
    ppermute x2, starting transfers between devices, swapped(): return lax.ppermute(block, axis, [(i, i ^ 1 << bit) for i in range(count)])  1.73 us
    pallas_call x1, Pallas kernels, gather(): pl.pallas_call(functools.partial(gather_kernel, tile_count, row_share), i...  1.36 us
  transfers between devices with their start and end apart: 9, of which 6 were waited for; matrix products, arithmetic and copies ran while one was open for 0% of the time, Pallas kernels for 0%

profile of v3, /device:TPU:0, one launch (start us, length us, event | category | flops | bytes accessed | tf_op | source)
XLA Modules:
  0.0 59.6 jit_solution(12203476312053951950)
XLA Ops:
  0.0 0.0 copy-start.1
  0.0 0.0 copy-start.4
  0.0 0.0 copy-start.3
  0.0 0.6 pad_add_fusion.refs_3_.refs_1_
  0.6 0.0 copy-start.2
  0.6 9.8 %march.1 = (s16[8,4,8,128]{3,2,1,0:T(8,128)(2,1)}, s16[8,4,8,128]{3,2,1,0:T(8,128)(2,1)}, s16[8,4,8,128]{3,2,1,0:T(8,128)(2,1)}, s16[8,4,8,128]{3,2,1,0:T(8,128)...) custom-call(s32[8]{0:T(128)} %bitcast.6, ...), custom_call_target="tpu_custom_call" | custom-call | tf_op jit(solution)/shard_map/march/pallas_call | solution.py:147
  10.4 6.4 %collective-permute-start = (s16[8,4,8,128]{3,2,1,0:T(8,128)(2,1)}, s16[8,4,8,128]{3,2,1,0:T(8,128)(2,1)S(1)}, u32[]{:S(2)}, u32[]{:S(2)}) collective-permute-start(s16[8,4,8,128]{3,2,1,0:T(8,128)(2,1)} %get-tuple-element.18), channel_id=1, source_target_pairs={{0,4},{4,8},{8,12},{12,16},{16,20},{20,24},{24,28},{28,0},{1,5},{5... | collective-permute-start | bytes 196616 | tf_op jit(solution)/shard_map/ppermute | solution.py:304
  16.8 20.3 %collective-permute-start.1 = (s16[8,4,8,128]{3,2,1,0:T(8,128)(2,1)}, s16[8,4,8,128]{3,2,1,0:T(8,128)(2,1)S(1)}, u32[]{:S(2)}, u32[]{:S(2)}) collective-permute-start(s16[8,4,8,128]{3,2,1,0:T(8,128)(2,1)} %get-tuple-element.19), channel_id=1, source_target_pairs={{0,8},{4,12},{8,16},{12,20},{16,24},{20,28},{24,0},{28,4},{1,9},{5... | collective-permute-start | bytes 196616 | tf_op jit(solution)/shard_map/ppermute | solution.py:304
  37.2 0.0 collective-permute-start.2
  37.2 5.2 %collective-permute-start.3 = (s16[8,4,8,128]{3,2,1,0:T(8,128)(2,1)}, s16[8,4,8,128]{3,2,1,0:T(8,128)(2,1)S(1)}, u32[]{:S(2)}, u32[]{:S(2)}) collective-permute-start(s16[8,4,8,128]{3,2,1,0:T(8,128)(2,1)} %get-tuple-element.21), channel_id=1, source_target_pairs={{0,16},{4,20},{8,24},{12,28},{16,0},{20,4},{24,8},{28,12},{1,17},{... | collective-permute-start | bytes 196616 | tf_op jit(solution)/shard_map/ppermute | solution.py:304
  42.4 0.0 collective-permute-start.4
  42.4 0.0 collective-permute-done.refs_5_
  42.4 2.4 %collective-permute-start.5 = (s16[8,4,8,128]{3,2,1,0:T(8,128)(2,1)}, s16[8,4,8,128]{3,2,1,0:T(8,128)(2,1)S(1)}, u32[]{:S(2)}, u32[]{:S(2)}) collective-permute-start(s16[8,4,8,128]{3,2,1,0:T(8,128)(2,1)} %get-tuple-element.23), channel_id=1, source_target_pairs={{0,24},{4,28},{8,0},{12,4},{16,8},{20,12},{24,16},{28,20},{1,25},{... | collective-permute-start | bytes 196616 | tf_op jit(solution)/shard_map/ppermute | solution.py:304
  44.7 0.0 collective-permute-done.1.refs_6_
  44.8 1.5 %collective-permute-start.6 = (s16[8,4,8,128]{3,2,1,0:T(8,128)(2,1)}, s16[8,4,8,128]{3,2,1,0:T(8,128)(2,1)S(1)}, u32[]{:S(2)}, u32[]{:S(2)}) collective-permute-start(s16[8,4,8,128]{3,2,1,0:T(8,128)(2,1)} %get-tuple-element.24), channel_id=1, source_target_pairs={{0,28},{4,0},{8,4},{12,8},{16,12},{20,16},{24,20},{28,24},{1,29},{... | collective-permute-start | bytes 196616 | tf_op jit(solution)/shard_map/ppermute | solution.py:304
  46.2 1.6 %collective-permute-done.2.refs_7_ = s16[8,4,8,128]{3,2,1,0:T(8,128)(2,1)S(1)} collective-permute-done((s16[8,4,8,128]{3,2,1,0:T(8,128)(2,1)}, s16[8,4,8,128]{3,2,1,0:T(8,128)(2,1)S(1)}, u32[]{:S(2)}, u32[]{:S(2)}) %collective-permute-start.2) | collective-permute-done | bytes 65568 | tf_op jit(solution)/shard_map/ppermute | solution.py:304
  47.9 0.1 collective-permute-done.3.refs_8_
  48.0 0.6 collective-permute-done.4.refs_9_
  48.5 1.4 %collective-permute-done.5.refs_10_ = s16[8,4,8,128]{3,2,1,0:T(8,128)(2,1)S(1)} collective-permute-done((s16[8,4,8,128]{3,2,1,0:T(8,128)(2,1)}, s16[8,4,8,128]{3,2,1,0:T(8,128)(2,1)S(1)}, u32[]{:S(2)}, u32[]{:S(2)}) %collective-permute-start.5) | collective-permute-done | bytes 65568 | tf_op jit(solution)/shard_map/ppermute | solution.py:304
  49.9 0.0 collective-permute-done.6.refs_11_
  49.9 0.0 copy-done.1
  49.9 0.0 copy-done.4
  49.9 0.0 copy-done.3
  49.9 0.0 copy-done.2
  49.9 0.0 copy-start
  49.9 0.8 %copy-done = s16[8,4,8,128]{3,2,1,0:T(8,128)(2,1)S(1)} copy-done((s16[8,4,8,128]{3,2,1,0:T(8,128)(2,1)S(1)}, s16[8,4,8,128]{3,2,1,0:T(8,128)(2,1)}, u32[]{:S(2)}) %copy-start) | copy-done | bytes 65560
  50.8 1.4 %gather.1 = (f32[4,64,128]{2,1,0:T(8,128)S(1)}, f32[4,64,128]{2,1,0:T(8,128)S(1)}) custom-call(s32[8]{0:T(128)S(1)} %bitcast.7, s32[8]{0:T(128)S(1)} %bitcast.9, s32[8]{0:T(128)S(1)} %copy-done.1, s32[2]{0:T(128)S(1)} %copy-done.2, s16[8,4,8,128]{3,2,1,0:T(8,128)(2,1)S(1)} %copy-done, s16[8,4,8,128]{3,2,1,0:T(8,128)(2,1)S(1)} %collective-permute-done.refs_5_, ...), custom_call_target="tpu_custom_call" | custom-call | tf_op jit(solution)/shard_map/gather/pallas_call | solution.py:234
  52.1 0.1 collective-permute-start.7
  52.2 1.3 %collective-permute-done.7.refs_3_ = f32[4,64,128]{2,1,0:T(8,128)S(1)} collective-permute-done((f32[4,64,128]{2,1,0:T(8,128)S(1)}, f32[4,64,128]{2,1,0:T(8,128)S(1)}, u32[]{:S(2)}, u32[]{:S(2)}) %collective-permute-start.7) | collective-permute-done | bytes 131104 | tf_op jit(solution)/shard_map/ppermute | solution.py:291
  53.5 0.6 blend.2
  54.1 1.7 %collective-permute-start.8 = (f32[4,32,128]{2,1,0:T(8,128)S(1)}, f32[4,32,128]{2,1,0:T(8,128)S(1)}, u32[]{:S(2)}, u32[]{:S(2)}) collective-permute-start(f32[4,32,128]{2,1,0:T(8,128)S(1)} %get-tuple-element.28), channel_id=1, source_target_pairs={{0,2},{1,3},{2,0},{3,1},{4,6},{5,7},{6,4},{7,5},{8,10},{9,11},{10,... | collective-permute-start | bytes 196616 | tf_op jit(solution)/shard_map/ppermute | solution.py:291
  55.8 2.7 %collective-permute-done.8.refs_3_ = f32[4,32,128]{2,1,0:T(8,128)S(1)} collective-permute-done((f32[4,32,128]{2,1,0:T(8,128)S(1)}, f32[4,32,128]{2,1,0:T(8,128)S(1)}, u32[]{:S(2)}, u32[]{:S(2)}) %collective-permute-start.8) | collective-permute-done | bytes 65568 | tf_op jit(solution)/shard_map/ppermute | solution.py:291
  58.5 1.2 %blend.3 = f32[4,32,128]{2,1,0:T(8,128)} custom-call(s32[8]{0:T(128)S(1)} %copy-done.1, s32[2]{0:T(128)S(1)} %copy-done.2, f32[4,32,128]{2,1,0:T(8,128)S(1)} %get-tuple-element.27.refs_2_, f32[4,32,128]{2,1,0:T(8,128)S(1)} %collective-permute-done.8.refs_3_), custom_call_target="tpu_custom_call" | custom-call | tf_op jit(solution)/shard_map/blend/pallas_call | solution.py:278
Async XLA Ops:
  0.0 49.9 %copy-start.1 = (s32[8]{0:T(128)S(1)}, s32[8]{0:T(128)}, u32[]{:S(2)}) copy-start(s32[8]{0:T(128)} %refs_0_.3) | copy-start | bytes 100
  0.0 49.9 %copy-start.4 = (s32[1,8]{1,0:T(1,128)S(1)}, s32[1,8]{1,0:T(1,128)}, u32[]{:S(2)}) copy-start(s32[1,8]{1,0:T(1,128)} %param.8) | copy-start | bytes 100
  0.0 49.9 %copy-start.3 = (s32[1,8]{1,0:T(1,128)S(1)}, s32[1,8]{1,0:T(1,128)}, u32[]{:S(2)}) copy-start(s32[1,8]{1,0:T(1,128)} %param.7) | copy-start | bytes 100
  0.6 49.3 %copy-start.2 = (s32[2]{0:T(128)S(1)}, s32[2]{0:T(128)}, u32[]{:S(2)}) copy-start(s32[2]{0:T(128)} %pad_add_fusion.refs_3_.refs_1_) | copy-start | bytes 28
  10.4 32.0 %collective-permute-start = (s16[8,4,8,128]{3,2,1,0:T(8,128)(2,1)}, s16[8,4,8,128]{3,2,1,0:T(8,128)(2,1)S(1)}, u32[]{:S(2)}, u32[]{:S(2)}) collective-permute-start(s16[8,4,8,128]{3,2,1,0:T(8,128)(2,1)} %get-tuple-element.18), channel_id=1, source_target_pairs={{0,4},{4,8},{8,12},{12,16},{16,20},{20,24},{24,28},{28,0},{1,5},{5... | collective-permute-start | bytes 196616 | tf_op jit(solution)/shard_map/ppermute | solution.py:304
  16.8 27.9 %collective-permute-start.1 = (s16[8,4,8,128]{3,2,1,0:T(8,128)(2,1)}, s16[8,4,8,128]{3,2,1,0:T(8,128)(2,1)S(1)}, u32[]{:S(2)}, u32[]{:S(2)}) collective-permute-start(s16[8,4,8,128]{3,2,1,0:T(8,128)(2,1)} %get-tuple-element.19), channel_id=1, source_target_pairs={{0,8},{4,12},{8,16},{12,20},{16,24},{20,28},{24,0},{28,4},{1,9},{5... | collective-permute-start | bytes 196616 | tf_op jit(solution)/shard_map/ppermute | solution.py:304
  37.2 10.7 %collective-permute-start.2 = (s16[8,4,8,128]{3,2,1,0:T(8,128)(2,1)}, s16[8,4,8,128]{3,2,1,0:T(8,128)(2,1)S(1)}, u32[]{:S(2)}, u32[]{:S(2)}) collective-permute-start(s16[8,4,8,128]{3,2,1,0:T(8,128)(2,1)} %get-tuple-element.20), channel_id=1, source_target_pairs={{0,12},{4,16},{8,20},{12,24},{16,28},{20,0},{24,4},{28,8},{1,13},{... | collective-permute-start | bytes 196616 | tf_op jit(solution)/shard_map/ppermute | solution.py:304
  37.2 10.8 %collective-permute-start.3 = (s16[8,4,8,128]{3,2,1,0:T(8,128)(2,1)}, s16[8,4,8,128]{3,2,1,0:T(8,128)(2,1)S(1)}, u32[]{:S(2)}, u32[]{:S(2)}) collective-permute-start(s16[8,4,8,128]{3,2,1,0:T(8,128)(2,1)} %get-tuple-element.21), channel_id=1, source_target_pairs={{0,16},{4,20},{8,24},{12,28},{16,0},{20,4},{24,8},{28,12},{1,17},{... | collective-permute-start | bytes 196616 | tf_op jit(solution)/shard_map/ppermute | solution.py:304
  42.4 6.1 %collective-permute-start.4 = (s16[8,4,8,128]{3,2,1,0:T(8,128)(2,1)}, s16[8,4,8,128]{3,2,1,0:T(8,128)(2,1)S(1)}, u32[]{:S(2)}, u32[]{:S(2)}) collective-permute-start(s16[8,4,8,128]{3,2,1,0:T(8,128)(2,1)} %get-tuple-element.22), channel_id=1, source_target_pairs={{0,20},{4,24},{8,28},{12,0},{16,4},{20,8},{24,12},{28,16},{1,21},{... | collective-permute-start | bytes 196616 | tf_op jit(solution)/shard_map/ppermute | solution.py:304
  42.4 7.5 %collective-permute-start.5 = (s16[8,4,8,128]{3,2,1,0:T(8,128)(2,1)}, s16[8,4,8,128]{3,2,1,0:T(8,128)(2,1)S(1)}, u32[]{:S(2)}, u32[]{:S(2)}) collective-permute-start(s16[8,4,8,128]{3,2,1,0:T(8,128)(2,1)} %get-tuple-element.23), channel_id=1, source_target_pairs={{0,24},{4,28},{8,0},{12,4},{16,8},{20,12},{24,16},{28,20},{1,25},{... | collective-permute-start | bytes 196616 | tf_op jit(solution)/shard_map/ppermute | solution.py:304
  44.8 5.1 %collective-permute-start.6 = (s16[8,4,8,128]{3,2,1,0:T(8,128)(2,1)}, s16[8,4,8,128]{3,2,1,0:T(8,128)(2,1)S(1)}, u32[]{:S(2)}, u32[]{:S(2)}) collective-permute-start(s16[8,4,8,128]{3,2,1,0:T(8,128)(2,1)} %get-tuple-element.24), channel_id=1, source_target_pairs={{0,28},{4,0},{8,4},{12,8},{16,12},{20,16},{24,20},{28,24},{1,29},{... | collective-permute-start | bytes 196616 | tf_op jit(solution)/shard_map/ppermute | solution.py:304
  49.9 0.8 %copy-start = (s16[8,4,8,128]{3,2,1,0:T(8,128)(2,1)S(1)}, s16[8,4,8,128]{3,2,1,0:T(8,128)(2,1)}, u32[]{:S(2)}) copy-start(s16[8,4,8,128]{3,2,1,0:T(8,128)(2,1)} %get-tuple-element.17.refs_4_) | copy-start | bytes 196612
  52.1 1.4 %collective-permute-start.7 = (f32[4,64,128]{2,1,0:T(8,128)S(1)}, f32[4,64,128]{2,1,0:T(8,128)S(1)}, u32[]{:S(2)}, u32[]{:S(2)}) collective-permute-start(f32[4,64,128]{2,1,0:T(8,128)S(1)} %get-tuple-element.26), channel_id=1, source_target_pairs={{0,1},{1,0},{2,3},{3,2},{4,5},{5,4},{6,7},{7,6},{8,9},{9,8},{10,11... | collective-permute-start | bytes 393224 | tf_op jit(solution)/shard_map/ppermute | solution.py:291
  54.1 4.3 %collective-permute-start.8 = (f32[4,32,128]{2,1,0:T(8,128)S(1)}, f32[4,32,128]{2,1,0:T(8,128)S(1)}, u32[]{:S(2)}, u32[]{:S(2)}) collective-permute-start(f32[4,32,128]{2,1,0:T(8,128)S(1)} %get-tuple-element.28), channel_id=1, source_target_pairs={{0,2},{1,3},{2,0},{3,1},{4,6},{5,7},{6,4},{7,5},{8,10},{9,11},{10,... | collective-permute-start | bytes 196616 | tf_op jit(solution)/shard_map/ppermute | solution.py:291

commit v4 on v3

--- a/solution.py
+++ b/solution.py
@@ -23,8 +23,10 @@
 CODE_MID = 32767.5
 GRANT = 12 << 20
 MARCH_GRANT = 61 << 20
-WIDE = 2
-UNROLL = 16
+SPAN = 1024
+GROUPS = PIXELS // SPAN
+STACK = 8 * GROUPS
+PACK = 16 // 8
 
 
 def exclusive_start(counts_ref, index, tile_count):
@@ -56,7 +58,7 @@
 def march_kernel(step_size, tile_count, relative, *refs):
     counts_ref, order_ref, flip_ref, me_ref, center_ref, amp_ref, cells_ref = refs[:7]
     outs = refs[7:7 + relative]
-    coef_ref, stage_ref = refs[7 + relative:]
+    coef_ref, mix_ref, stage_ref, slot_ref = refs[7 + relative:]
     step = pl.program_id(0)
     me = me_ref[0]
     start = exclusive_start(counts_ref, me, tile_count)
@@ -64,74 +66,96 @@
 
     @pl.when(step == 0)
     def _():
+        for r in range(relative):
+            tile = lax.rem(me + r, tile_count)
+            slot_ref[r] = lax.rem(
+                position_of(order_ref, tile, tile_count) - start + tile_count * 64, tile_count
+            )
         w = center_ref[...] * ROOT
         folded = amp_ref[...] * jnp.exp2(-w * w)
+        channel = lax.broadcasted_iota(jnp.int32, (4, 1), 0)
+        folded = folded * jnp.where(channel == 3, LOG2E, 0.5)
         for k in range(KNOTS):
             coef_ref[k] = jnp.broadcast_to(2.0 * w[:, k:k + 1], (8, LANES))
+        knot = lax.broadcasted_iota(jnp.int32, (4, KNOTS * STACK), 1) // STACK
+        spread = jnp.zeros((4, KNOTS * STACK), jnp.float32)
+        for k in range(KNOTS):
+            spread = jnp.where(knot == k, folded[:, k:k + 1], spread)
+        coarse = spread.astype(jnp.bfloat16)
+        fine = (spread - coarse.astype(jnp.float32)).astype(jnp.bfloat16)
+        own = lax.broadcasted_iota(jnp.int32, (STACK, KNOTS * STACK), 0) == lax.rem(
+            lax.broadcasted_iota(jnp.int32, (STACK, KNOTS * STACK), 1), STACK
+        )
+        width = KNOTS * STACK
+        for part, amps in enumerate((coarse, fine, coarse)):
+            amps = amps.astype(jnp.float32)
             for c in range(4):
-                scale = LOG2E if c == 3 else 0.5
-                coef_ref[KNOTS + 4 * k + c] = jnp.broadcast_to(
-                    folded[c:c + 1, k:k + 1] * scale, (8, LANES)
-                )
+                line = jnp.where(own, amps[c:c + 1], 0.0)
+                mix_ref[c * STACK:(c + 1) * STACK, part * width:(part + 1) * width] = line.astype(jnp.bfloat16)
 
     @pl.when(step * tile_count < live)
     def _():
-        row = lax.broadcasted_iota(jnp.int32, (8, LANES), 0)
+        row = lax.broadcasted_iota(jnp.int32, (8, SPAN), 0)
         for half in range(tile_count // 8):
-            flip = jnp.zeros((8, LANES), jnp.int32)
+            flip = jnp.zeros((8, SPAN), jnp.int32)
             for s in range(8):
                 tile = order_ref[lax.rem(start + half * 8 + s, tile_count)]
                 flip = jnp.where(row == s, flip_ref[tile], flip)
             down = flip == 1
             signed_step = jnp.where(down, step_size * LOG2E, -step_size * LOG2E)
 
-            def columns(group, carry, half=half, down=down, signed_step=signed_step):
-                base = group * (WIDE * LANES)
-
-                def depth(z, state):
-                    lane = pl.multiple_of(z * PIXELS + base, LANES)
-                    raw = cells_ref[half * 8:half * 8 + 8, pl.ds(lane, WIDE * LANES)]
-                    values = raw.astype(jnp.float32) * ROOT
-                    after = []
-                    for j in range(WIDE):
-                        v = values[:, j * LANES:(j + 1) * LANES]
-                        total, seen, reds, greens, blues = state[j]
-                        fields = [None] * 4
-                        for k in range(KNOTS):
-                            bump = jnp.exp2(v * (coef_ref[k] - v))
-                            for c in range(4):
-                                term = coef_ref[KNOTS + 4 * k + c] * bump
-                                fields[c] = term if k == 0 else fields[c] + term
-                        total = total + jnp.log(1.0 + jnp.exp2(fields[3]))
-                        now = jnp.exp2(signed_step * total)
-                        weight = now - seen
-                        after.append((
-                            total,
-                            now,
-                            reds + weight * jnp.tanh(fields[0]),
-                            greens + weight * jnp.tanh(fields[1]),
-                            blues + weight * jnp.tanh(fields[2]),
-                        ))
-                    return tuple(after)
-
-                zero = jnp.zeros((8, LANES), jnp.float32)
-                first = tuple((zero, zero + 1.0, zero, zero, zero) for j in range(WIDE))
-                last = lax.fori_loop(0, BLOCK, depth, first, unroll=UNROLL)
-                for j in range(WIDE):
-                    total, seen, reds, greens, blues = last[j]
-                    passed = jnp.exp2(total * (-step_size * LOG2E))
-                    factor = jnp.where(down, 0.5 * passed, -0.5)
-                    spread = seen - 1.0
-                    rows = pl.ds(group * WIDE + j, 8, stride=TILES)
-                    for c, color in enumerate((reds, greens, blues)):
-                        stage_ref[half, c, rows, :] = factor * (spread + color)
-                    stage_ref[half, 3, rows, :] = 1.0 - passed
-                return carry
-
-            lax.fori_loop(0, TILES // WIDE, columns, 0)
+            def depth(z, state, half=half, signed_step=signed_step):
+                values = []
+                for j in range(GROUPS):
+                    lane = pl.multiple_of(z * PIXELS + j * SPAN, LANES)
+                    raw = cells_ref[half * 8:half * 8 + 8, pl.ds(lane, SPAN)]
+                    values.append(raw.astype(jnp.float32) * ROOT)
+                bumps = []
+                for k in range(KNOTS):
+                    center = jnp.concatenate([coef_ref[k]] * (SPAN // LANES), axis=1)
+                    bumps += [jnp.exp2(v * (center - v)) for v in values]
+                high, low = [], []
+                for n in range(0, len(bumps), PACK):
+                    bump = jnp.concatenate(bumps[n:n + PACK], axis=0)
+                    coarse = bump.astype(jnp.bfloat16)
+                    high.append(coarse)
+                    low.append((bump - coarse.astype(jnp.float32)).astype(jnp.bfloat16))
+                stacked = jnp.concatenate(high + high + low, axis=0)
+                fields = jnp.dot(mix_ref[...], stacked, preferred_element_type=jnp.float32)
+                after = []
+                for j in range(GROUPS):
+                    red, green, blue, dense = (
+                        fields[c * STACK + j * 8:c * STACK + j * 8 + 8] for c in range(4)
+                    )
+                    total, seen, reds, greens, blues = state[j]
+                    total = total + jnp.log(1.0 + jnp.exp2(dense))
+                    now = jnp.exp2(signed_step * total)
+                    weight = now - seen
+                    after.append((
+                        total,
+                        now,
+                        reds + weight * jnp.tanh(red),
+                        greens + weight * jnp.tanh(green),
+                        blues + weight * jnp.tanh(blue),
+                    ))
+                return tuple(after)
+
+            zero = jnp.zeros((8, SPAN), jnp.float32)
+            first = tuple((zero, zero + 1.0, zero, zero, zero) for j in range(GROUPS))
+            last = lax.fori_loop(0, BLOCK, depth, first, unroll=True)
+            for j in range(GROUPS):
+                total, seen, reds, greens, blues = last[j]
+                passed = jnp.exp2(total * (-step_size * LOG2E))
+                factor = jnp.where(down, 0.5 * passed, -0.5)
+                spread = seen - 1.0
+                planes = [factor * (spread + color) for color in (reds, greens, blues)]
+                planes.append(1.0 - passed)
+                for c in range(4):
+                    for i in range(SPAN // LANES):
+                        rows = pl.ds(j * (SPAN // LANES) + i, 8, stride=TILES)
+                        stage_ref[half, c, rows, :] = planes[c][:, i * LANES:(i + 1) * LANES]
         for r in range(relative):
-            tile = lax.rem(me + r, tile_count)
-            slot = lax.rem(position_of(order_ref, tile, tile_count) - start + tile_count * 64, tile_count)
+            slot = slot_ref[r]
             rows = pl.ds(pl.multiple_of(lax.rem(slot, 8) * TILES, TILES), TILES)
             for c in range(4):
                 outs[r][0, c] = encode(stage_ref[slot // 8, c, rows, :])
@@ -155,8 +179,10 @@
         out_specs=[block] * tile_count,
         out_shape=[jax.ShapeDtypeStruct((capacity, 4, TILES, LANES), jnp.int16)] * tile_count,
         scratch_shapes=[
-            pltpu.VMEM((KNOTS * 5, 8, LANES), jnp.float32),
+            pltpu.VMEM((KNOTS, 8, LANES), jnp.float32),
+            pltpu.VMEM((4 * STACK, 3 * KNOTS * STACK), jnp.bfloat16),
             pltpu.VMEM((tile_count // 8, 4, 8 * TILES, LANES), jnp.float32),
+            pltpu.SMEM((tile_count,), jnp.int32),
         ],
         compiler_params=pltpu.CompilerParams(vmem_limit_bytes=MARCH_GRANT),
         name="march",
@@ -173,15 +199,19 @@
 
 
 def gather_kernel(tile_count, row_share, *refs):
-    counts_ref, order_ref, flip_ref, me_ref = refs[:4]
-    arrived = refs[4:4 + tile_count]
-    kept_ref, given_ref, brick_ref, image_ref = refs[4 + tile_count:]
+    counts_ref, order_ref, flip_ref, me_ref, layer_ref, home_ref = refs[:6]
+    kept_ref, given_ref, brick_ref, image_ref, own_ref, own_sem = refs[5 + tile_count:]
+    arrived = (own_ref,) + refs[6:5 + tile_count]
+    own_copy = pltpu.make_async_copy(home_ref, own_ref, own_sem)
+    own_copy.start()
     me = me_ref[0]
     position = position_of(order_ref, me, tile_count)
     starts = [jnp.int32(0)]
     for i in range(tile_count):
         starts.append(starts[-1] + counts_ref[i])
-    for r in range(tile_count):
+    for r in [*range(1, tile_count), 0]:
+        if r == 0:
+            own_copy.wait()
         owner = lax.rem(me - r + tile_count, tile_count)
         start = jnp.int32(0)
         for i in range(tile_count):
@@ -222,10 +252,10 @@
                         moved = pltpu.roll(moved, turn, 1)
                     line = moved if line is None else jnp.where(lane == bx, moved, line)
                 image_ref[c, pl.ds(by * BLOCK + s, TILES, stride=per_row), :] = line
-    split_rows(image_ref, kept_ref, given_ref, me_ref[1] & 1, row_share)
-
-
-def gather(counts, order, flip, me, arrived, row_share):
+    split_rows(image_ref, kept_ref, given_ref, layer_ref[0] & 1, row_share)
+
+
+def gather(counts, order, flip, me, layer, arrived, row_share):
     tile_count = counts.shape[0]
     scalar = pl.BlockSpec(memory_space=pltpu.SMEM)
     vmem = pl.BlockSpec(memory_space=pltpu.VMEM)
@@ -233,23 +263,25 @@
     half = jax.ShapeDtypeStruct((4, rows // 2, width), jnp.float32)
     return pl.pallas_call(
         functools.partial(gather_kernel, tile_count, row_share),
-        in_specs=[scalar] * 4 + [vmem] * tile_count,
+        in_specs=[scalar] * 5 + [pl.BlockSpec(memory_space=pltpu.HBM)] + [vmem] * (tile_count - 1),
         out_specs=[vmem] * 2,
         out_shape=[half, half],
         scratch_shapes=[
             pltpu.VMEM((DB * BY * BX, 4, TILES, LANES), jnp.float32),
             pltpu.VMEM((4, rows, width), jnp.float32),
+            pltpu.VMEM(arrived[0].shape, arrived[0].dtype),
+            pltpu.SemaphoreType.DMA,
         ],
         compiler_params=pltpu.CompilerParams(vmem_limit_bytes=GRANT),
         name="gather",
-    )(counts, order, flip, me, *arrived)
+    )(counts, order, flip, me, layer, *arrived)
 
 
 def blend_kernel(bit, row_share, *refs):
-    flip_ref, me_ref, kept_ref, other_ref = refs[:4]
-    side = me_ref[1] >> bit & 1
+    flip_ref, me_ref, layer_ref, kept_ref, other_ref = refs[:5]
+    side = layer_ref[0] >> bit & 1
     front = side == flip_ref[me_ref[0]]
-    last = len(refs) == 5
+    last = len(refs) == 6
     out_ref = refs[-1]
 
     def blend(near_ref, far_ref):
@@ -266,10 +298,10 @@
         blend(other_ref, kept_ref)
 
     if not last:
-        split_rows(out_ref, refs[4], refs[5], me_ref[1] >> (bit + 1) & 1, row_share)
-
-
-def blend(flip, me, kept, other, bit, row_share):
+        split_rows(out_ref, refs[5], refs[6], layer_ref[0] >> (bit + 1) & 1, row_share)
+
+
+def blend(flip, me, layer, kept, other, bit, row_share):
     scalar = pl.BlockSpec(memory_space=pltpu.SMEM)
     vmem = pl.BlockSpec(memory_space=pltpu.VMEM)
     last = kept.shape[1] == row_share
@@ -277,13 +309,13 @@
     half = jax.ShapeDtypeStruct((4, kept.shape[1] // 2, kept.shape[2]), jnp.float32)
     return pl.pallas_call(
         functools.partial(blend_kernel, bit, row_share),
-        in_specs=[scalar] * 2 + [vmem] * 2,
+        in_specs=[scalar] * 3 + [vmem] * 2,
         out_specs=vmem if last else [vmem] * 2,
         out_shape=whole if last else [half, half],
         scratch_shapes=[] if last else [pltpu.VMEM(kept.shape, jnp.float32)],
         compiler_params=pltpu.CompilerParams(vmem_limit_bytes=GRANT),
         name="blend",
-    )(flip, me, kept, other)
+    )(flip, me, layer, kept, other)
 
 
 def swapped(block, axis, bit):
@@ -295,7 +327,8 @@
     tile_count = lax.axis_size("tile")
     depth_count = lax.axis_size("depth")
     step_size = 1.5 / (depth_count * DB * BLOCK)
-    me = jnp.stack([lax.axis_index("tile"), lax.axis_index("depth")]).astype(jnp.int32)
+    me = lax.axis_index("tile").astype(jnp.int32).reshape(1)
+    layer = lax.axis_index("depth").astype(jnp.int32).reshape(1)
     counts, order = slot_counts[0], brick_order[0]
     sent = march(counts, order, view_flip, me, tf_centers, tf_amps, owned_blocks[0], step_size)
     arrived = [sent[0]]
@@ -303,11 +336,11 @@
         route = [(i, (i + r) % tile_count) for i in range(tile_count)]
         arrived.append(lax.ppermute(sent[r], "tile", route))
     row_share = BY * BLOCK // depth_count
-    kept, given = gather(counts, order, view_flip, me, arrived, row_share)
+    kept, given = gather(counts, order, view_flip, me, layer, arrived, row_share)
     levels = depth_count.bit_length() - 1
     for bit in range(levels):
         other = swapped(given, "depth", bit)
-        blended = blend(view_flip, me, kept, other, bit, row_share)
+        blended = blend(view_flip, me, layer, kept, other, bit, row_share)
         if bit < levels - 1:
             kept, given = blended
     return blended

time: 59.7 us -> 55.3 us (0.926)
  starting transfers between devices: 37.6 us -> 32.5 us
  waiting for transfers between devices: 7.67 us -> 8.81 us
    ppermute x7, starting transfers between devices: 35.8 us -> 31.9 us  [body(): arrived.append(lax.ppermute(sent[r], 'tile', route))]
    ppermute x2, waiting for transfers between devices: 4.01 us -> 5.14 us  [swapped(): return lax.ppermute(block, axis, [(i, i ^ 1 << bit) for i in range(count)])]
    ppermute x2, starting transfers between devices: 1.73 us -> 0.6 us  [swapped(): return lax.ppermute(block, axis, [(i, i ^ 1 << bit) for i in range(count)])]
where the time goes in v4:
time: 55.3 us; the launch traced here: 54.7 us
  starting transfers between devices  32.5 us (59%)
  Pallas kernels  12.5 us (23%)
  waiting for transfers between devices  8.81 us (16%)
  local copies, waits for them, and re-layouts  0.85 us (2%)
    ppermute x7, starting transfers between devices, body(): arrived.append(lax.ppermute(sent[r], 'tile', route))  31.9 us
    pallas_call x1, Pallas kernels, march(): pl.pallas_call(functools.partial(march_kernel, step_size, tile_count, til...  9.27 us
    ppermute x2, waiting for transfers between devices, swapped(): return lax.ppermute(block, axis, [(i, i ^ 1 << bit) for i in range(count)])  5.14 us
    ppermute x7, waiting for transfers between devices, body(): arrived.append(lax.ppermute(sent[r], 'tile', route))  3.67 us
    pallas_call x2, Pallas kernels, blend(): pl.pallas_call(functools.partial(blend_kernel, bit, row_share), in_specs=...  1.77 us
    pallas_call x1, Pallas kernels, gather(): pl.pallas_call(functools.partial(gather_kernel, tile_count, row_share), i...  1.44 us
  transfers between devices with their start and end apart: 9, of which 6 were waited for; matrix products, arithmetic and copies ran while one was open for 0% of the time, Pallas kernels for 0%

profile of v4, /device:TPU:0, one launch (start us, length us, event | category | flops | bytes accessed | tf_op | source)
XLA Modules:
  0.0 54.7 jit_solution(14328839073404161450)
XLA Ops:
  0.0 0.0 copy-start.1
  0.0 0.0 copy-start.3
  0.0 0.0 copy-start.2
  0.0 9.3 %march.1 = (s16[8,4,8,128]{3,2,1,0:T(8,128)(2,1)}, s16[8,4,8,128]{3,2,1,0:T(8,128)(2,1)}, s16[8,4,8,128]{3,2,1,0:T(8,128)(2,1)}, s16[8,4,8,128]{3,2,1,0:T(8,128)...) custom-call(s32[8]{0:T(128)} %bitcast.6, ...), custom_call_target="tpu_custom_call" | custom-call | tf_op jit(solution)/shard_map/march/pallas_call | solution.py:171
  9.3 3.1 %collective-permute-start = (s16[8,4,8,128]{3,2,1,0:T(8,128)(2,1)}, s16[8,4,8,128]{3,2,1,0:T(8,128)(2,1)S(1)}, u32[]{:S(2)}, u32[]{:S(2)}) collective-permute-start(s16[8,4,8,128]{3,2,1,0:T(8,128)(2,1)} %get-tuple-element.18), channel_id=1, source_target_pairs={{0,4},{4,8},{8,12},{12,16},{16,20},{20,24},{24,28},{28,0},{1,5},{5... | collective-permute-start | bytes 196616 | tf_op jit(solution)/shard_map/ppermute | solution.py:337
  12.3 19.8 %collective-permute-start.1 = (s16[8,4,8,128]{3,2,1,0:T(8,128)(2,1)}, s16[8,4,8,128]{3,2,1,0:T(8,128)(2,1)S(1)}, u32[]{:S(2)}, u32[]{:S(2)}) collective-permute-start(s16[8,4,8,128]{3,2,1,0:T(8,128)(2,1)} %get-tuple-element.19), channel_id=1, source_target_pairs={{0,8},{4,12},{8,16},{12,20},{16,24},{20,28},{24,0},{28,4},{1,9},{5... | collective-permute-start | bytes 196616 | tf_op jit(solution)/shard_map/ppermute | solution.py:337
  32.2 0.0 collective-permute-start.2
  32.2 5.2 %collective-permute-start.3 = (s16[8,4,8,128]{3,2,1,0:T(8,128)(2,1)}, s16[8,4,8,128]{3,2,1,0:T(8,128)(2,1)S(1)}, u32[]{:S(2)}, u32[]{:S(2)}) collective-permute-start(s16[8,4,8,128]{3,2,1,0:T(8,128)(2,1)} %get-tuple-element.21), channel_id=1, source_target_pairs={{0,16},{4,20},{8,24},{12,28},{16,0},{20,4},{24,8},{28,12},{1,17},{... | collective-permute-start | bytes 196616 | tf_op jit(solution)/shard_map/ppermute | solution.py:337
  37.4 0.0 collective-permute-start.4
  37.4 0.0 collective-permute-done.refs_6_
  37.4 2.4 %collective-permute-start.5 = (s16[8,4,8,128]{3,2,1,0:T(8,128)(2,1)}, s16[8,4,8,128]{3,2,1,0:T(8,128)(2,1)S(1)}, u32[]{:S(2)}, u32[]{:S(2)}) collective-permute-start(s16[8,4,8,128]{3,2,1,0:T(8,128)(2,1)} %get-tuple-element.23), channel_id=1, source_target_pairs={{0,24},{4,28},{8,0},{12,4},{16,8},{20,12},{24,16},{28,20},{1,25},{... | collective-permute-start | bytes 196616 | tf_op jit(solution)/shard_map/ppermute | solution.py:337
  39.8 0.0 collective-permute-done.1.refs_7_
  39.8 1.5 %collective-permute-start.6 = (s16[8,4,8,128]{3,2,1,0:T(8,128)(2,1)}, s16[8,4,8,128]{3,2,1,0:T(8,128)(2,1)S(1)}, u32[]{:S(2)}, u32[]{:S(2)}) collective-permute-start(s16[8,4,8,128]{3,2,1,0:T(8,128)(2,1)} %get-tuple-element.24), channel_id=1, source_target_pairs={{0,28},{4,0},{8,4},{12,8},{16,12},{20,16},{24,20},{28,24},{1,29},{... | collective-permute-start | bytes 196616 | tf_op jit(solution)/shard_map/ppermute | solution.py:337
  41.2 1.6 %collective-permute-done.2.refs_8_ = s16[8,4,8,128]{3,2,1,0:T(8,128)(2,1)S(1)} collective-permute-done((s16[8,4,8,128]{3,2,1,0:T(8,128)(2,1)}, s16[8,4,8,128]{3,2,1,0:T(8,128)(2,1)S(1)}, u32[]{:S(2)}, u32[]{:S(2)}) %collective-permute-start.2) | collective-permute-done | bytes 65568 | tf_op jit(solution)/shard_map/ppermute | solution.py:337
  42.9 0.1 collective-permute-done.3.refs_9_
  43.0 0.6 %collective-permute-done.4.refs_10_ = s16[8,4,8,128]{3,2,1,0:T(8,128)(2,1)S(1)} collective-permute-done((s16[8,4,8,128]{3,2,1,0:T(8,128)(2,1)}, s16[8,4,8,128]{3,2,1,0:T(8,128)(2,1)S(1)}, u32[]{:S(2)}, u32[]{:S(2)}) %collective-permute-start.4) | collective-permute-done | bytes 65568 | tf_op jit(solution)/shard_map/ppermute | solution.py:337
  43.5 1.4 %collective-permute-done.5.refs_11_ = s16[8,4,8,128]{3,2,1,0:T(8,128)(2,1)S(1)} collective-permute-done((s16[8,4,8,128]{3,2,1,0:T(8,128)(2,1)}, s16[8,4,8,128]{3,2,1,0:T(8,128)(2,1)S(1)}, u32[]{:S(2)}, u32[]{:S(2)}) %collective-permute-start.5) | collective-permute-done | bytes 65568 | tf_op jit(solution)/shard_map/ppermute | solution.py:337
  44.9 0.0 collective-permute-done.6.refs_12_
  44.9 0.0 copy-done.1
  44.9 0.0 copy-done.3
  44.9 0.0 copy-done.2
  44.9 0.0 copy-start
  44.9 0.8 %copy-done = s16[8,4,8,128]{3,2,1,0:T(8,128)(2,1)S(1)} copy-done((s16[8,4,8,128]{3,2,1,0:T(8,128)(2,1)S(1)}, s16[8,4,8,128]{3,2,1,0:T(8,128)(2,1)}, u32[]{:S(2)}) %copy-start) | copy-done | bytes 65560
  45.8 1.4 %gather.1 = (f32[4,64,128]{2,1,0:T(8,128)S(1)}, f32[4,64,128]{2,1,0:T(8,128)S(1)}) custom-call(s32[8]{0:T(128)S(1)} %bitcast.7, s32[8]{0:T(128)S(1)} %bitcast.9, s32[8]{0:T(128)S(1)} %copy-done.1, s32[1]{0:T(128)} %bitcast.refs_3_.refs_1_, s32[1]{0:T(128)} %bitcast.1.refs_4_.refs_2_, s16[8,4,8,128]{3,2,1,0:T(8,128)(2,1)S(1)} %copy-done, ...), custom_call_target="tpu_custom_call" | custom-call | tf_op jit(solution)/shard_map/gather/pallas_call | solution.py:264
  47.2 0.1 collective-permute-start.7
  47.3 1.3 %collective-permute-done.7.refs_4_ = f32[4,64,128]{2,1,0:T(8,128)S(1)} collective-permute-done((f32[4,64,128]{2,1,0:T(8,128)S(1)}, f32[4,64,128]{2,1,0:T(8,128)S(1)}, u32[]{:S(2)}, u32[]{:S(2)}) %collective-permute-start.7) | collective-permute-done | bytes 131104 | tf_op jit(solution)/shard_map/ppermute | solution.py:323
  48.6 0.6 %blend.2 = (f32[4,32,128]{2,1,0:T(8,128)S(1)}, f32[4,32,128]{2,1,0:T(8,128)S(1)}) custom-call(s32[8]{0:T(128)S(1)} %copy-done.1, s32[1]{0:T(128)} %bitcast.refs_3_.refs_1_, s32[1]{0:T(128)} %bitcast.1.refs_4_.refs_2_, f32[4,64,128]{2,1,0:T(8,128)S(1)} %get-tuple-element.25.refs_3_, f32[4,64,128]{2,1,0:T(8,128)S(1)} %collective-permute-done.7.refs_4_), custom_call_target="tpu_custom_call" | custom-call | tf_op jit(solution)/shard_map/blend/pallas_call | solution.py:310
  49.2 0.5 collective-permute-start.8
  49.7 3.8 %collective-permute-done.8.refs_4_ = f32[4,32,128]{2,1,0:T(8,128)S(1)} collective-permute-done((f32[4,32,128]{2,1,0:T(8,128)S(1)}, f32[4,32,128]{2,1,0:T(8,128)S(1)}, u32[]{:S(2)}, u32[]{:S(2)}) %collective-permute-start.8) | collective-permute-done | bytes 65568 | tf_op jit(solution)/shard_map/ppermute | solution.py:323
  53.5 1.2 %blend.3 = f32[4,32,128]{2,1,0:T(8,128)} custom-call(s32[8]{0:T(128)S(1)} %copy-done.1, s32[1]{0:T(128)} %bitcast.refs_3_.refs_1_, s32[1]{0:T(128)} %bitcast.1.refs_4_.refs_2_, f32[4,32,128]{2,1,0:T(8,128)S(1)} %get-tuple-element.27.refs_3_, f32[4,32,128]{2,1,0:T(8,128)S(1)} %collective-permute-done.8.refs_4_), custom_call_target="tpu_custom_call" | custom-call | tf_op jit(solution)/shard_map/blend/pallas_call | solution.py:310
Async XLA Ops:
  0.0 44.9 %copy-start.1 = (s32[8]{0:T(128)S(1)}, s32[8]{0:T(128)}, u32[]{:S(2)}) copy-start(s32[8]{0:T(128)} %refs_0_.3) | copy-start | bytes 100
  0.0 44.9 %copy-start.3 = (s32[1,8]{1,0:T(1,128)S(1)}, s32[1,8]{1,0:T(1,128)}, u32[]{:S(2)}) copy-start(s32[1,8]{1,0:T(1,128)} %param.8) | copy-start | bytes 100
  0.0 44.9 %copy-start.2 = (s32[1,8]{1,0:T(1,128)S(1)}, s32[1,8]{1,0:T(1,128)}, u32[]{:S(2)}) copy-start(s32[1,8]{1,0:T(1,128)} %param.7) | copy-start | bytes 100
  9.3 28.1 %collective-permute-start = (s16[8,4,8,128]{3,2,1,0:T(8,128)(2,1)}, s16[8,4,8,128]{3,2,1,0:T(8,128)(2,1)S(1)}, u32[]{:S(2)}, u32[]{:S(2)}) collective-permute-start(s16[8,4,8,128]{3,2,1,0:T(8,128)(2,1)} %get-tuple-element.18), channel_id=1, source_target_pairs={{0,4},{4,8},{8,12},{12,16},{16,20},{20,24},{24,28},{28,0},{1,5},{5... | collective-permute-start | bytes 196616 | tf_op jit(solution)/shard_map/ppermute | solution.py:337
  12.3 27.4 %collective-permute-start.1 = (s16[8,4,8,128]{3,2,1,0:T(8,128)(2,1)}, s16[8,4,8,128]{3,2,1,0:T(8,128)(2,1)S(1)}, u32[]{:S(2)}, u32[]{:S(2)}) collective-permute-start(s16[8,4,8,128]{3,2,1,0:T(8,128)(2,1)} %get-tuple-element.19), channel_id=1, source_target_pairs={{0,8},{4,12},{8,16},{12,20},{16,24},{20,28},{24,0},{28,4},{1,9},{5... | collective-permute-start | bytes 196616 | tf_op jit(solution)/shard_map/ppermute | solution.py:337
  32.2 10.7 %collective-permute-start.2 = (s16[8,4,8,128]{3,2,1,0:T(8,128)(2,1)}, s16[8,4,8,128]{3,2,1,0:T(8,128)(2,1)S(1)}, u32[]{:S(2)}, u32[]{:S(2)}) collective-permute-start(s16[8,4,8,128]{3,2,1,0:T(8,128)(2,1)} %get-tuple-element.20), channel_id=1, source_target_pairs={{0,12},{4,16},{8,20},{12,24},{16,28},{20,0},{24,4},{28,8},{1,13},{... | collective-permute-start | bytes 196616 | tf_op jit(solution)/shard_map/ppermute | solution.py:337
  32.2 10.8 %collective-permute-start.3 = (s16[8,4,8,128]{3,2,1,0:T(8,128)(2,1)}, s16[8,4,8,128]{3,2,1,0:T(8,128)(2,1)S(1)}, u32[]{:S(2)}, u32[]{:S(2)}) collective-permute-start(s16[8,4,8,128]{3,2,1,0:T(8,128)(2,1)} %get-tuple-element.21), channel_id=1, source_target_pairs={{0,16},{4,20},{8,24},{12,28},{16,0},{20,4},{24,8},{28,12},{1,17},{... | collective-permute-start | bytes 196616 | tf_op jit(solution)/shard_map/ppermute | solution.py:337
  37.4 6.1 %collective-permute-start.4 = (s16[8,4,8,128]{3,2,1,0:T(8,128)(2,1)}, s16[8,4,8,128]{3,2,1,0:T(8,128)(2,1)S(1)}, u32[]{:S(2)}, u32[]{:S(2)}) collective-permute-start(s16[8,4,8,128]{3,2,1,0:T(8,128)(2,1)} %get-tuple-element.22), channel_id=1, source_target_pairs={{0,20},{4,24},{8,28},{12,0},{16,4},{20,8},{24,12},{28,16},{1,21},{... | collective-permute-start | bytes 196616 | tf_op jit(solution)/shard_map/ppermute | solution.py:337
  37.4 7.5 %collective-permute-start.5 = (s16[8,4,8,128]{3,2,1,0:T(8,128)(2,1)}, s16[8,4,8,128]{3,2,1,0:T(8,128)(2,1)S(1)}, u32[]{:S(2)}, u32[]{:S(2)}) collective-permute-start(s16[8,4,8,128]{3,2,1,0:T(8,128)(2,1)} %get-tuple-element.23), channel_id=1, source_target_pairs={{0,24},{4,28},{8,0},{12,4},{16,8},{20,12},{24,16},{28,20},{1,25},{... | collective-permute-start | bytes 196616 | tf_op jit(solution)/shard_map/ppermute | solution.py:337
  39.8 5.1 %collective-permute-start.6 = (s16[8,4,8,128]{3,2,1,0:T(8,128)(2,1)}, s16[8,4,8,128]{3,2,1,0:T(8,128)(2,1)S(1)}, u32[]{:S(2)}, u32[]{:S(2)}) collective-permute-start(s16[8,4,8,128]{3,2,1,0:T(8,128)(2,1)} %get-tuple-element.24), channel_id=1, source_target_pairs={{0,28},{4,0},{8,4},{12,8},{16,12},{20,16},{24,20},{28,24},{1,29},{... | collective-permute-start | bytes 196616 | tf_op jit(solution)/shard_map/ppermute | solution.py:337
  44.9 0.8 %copy-start = (s16[8,4,8,128]{3,2,1,0:T(8,128)(2,1)S(1)}, s16[8,4,8,128]{3,2,1,0:T(8,128)(2,1)}, u32[]{:S(2)}) copy-start(s16[8,4,8,128]{3,2,1,0:T(8,128)(2,1)} %get-tuple-element.17.refs_5_) | copy-start | bytes 196612
  47.2 1.4 %collective-permute-start.7 = (f32[4,64,128]{2,1,0:T(8,128)S(1)}, f32[4,64,128]{2,1,0:T(8,128)S(1)}, u32[]{:S(2)}, u32[]{:S(2)}) collective-permute-start(f32[4,64,128]{2,1,0:T(8,128)S(1)} %get-tuple-element.26), channel_id=1, source_target_pairs={{0,1},{1,0},{2,3},{3,2},{4,5},{5,4},{6,7},{7,6},{8,9},{9,8},{10,11... | collective-permute-start | bytes 393224 | tf_op jit(solution)/shard_map/ppermute | solution.py:323
  49.2 4.3 %collective-permute-start.8 = (f32[4,32,128]{2,1,0:T(8,128)S(1)}, f32[4,32,128]{2,1,0:T(8,128)S(1)}, u32[]{:S(2)}, u32[]{:S(2)}) collective-permute-start(f32[4,32,128]{2,1,0:T(8,128)S(1)} %get-tuple-element.28), channel_id=1, source_target_pairs={{0,2},{1,3},{2,0},{3,1},{4,6},{5,7},{6,4},{7,5},{8,10},{9,11},{10,... | collective-permute-start | bytes 196616 | tf_op jit(solution)/shard_map/ppermute | solution.py:323

commit v5 on v4

--- a/solution.py
+++ b/solution.py
@@ -87,11 +87,13 @@
             lax.broadcasted_iota(jnp.int32, (STACK, KNOTS * STACK), 1), STACK
         )
         width = KNOTS * STACK
-        for part, amps in enumerate((coarse, fine, coarse)):
+        for part, amps in enumerate((coarse, fine)):
             amps = amps.astype(jnp.float32)
             for c in range(4):
-                line = jnp.where(own, amps[c:c + 1], 0.0)
-                mix_ref[c * STACK:(c + 1) * STACK, part * width:(part + 1) * width] = line.astype(jnp.bfloat16)
+                first = (part * 4 + c) * STACK
+                line = jnp.where(own, amps[c:c + 1], 0.0).astype(jnp.bfloat16)
+                mix_ref[first:first + STACK, :width] = line
+                mix_ref[first:first + STACK, width:] = line
 
     @pl.when(step * tile_count < live)
     def _():
@@ -120,8 +122,9 @@
                     coarse = bump.astype(jnp.bfloat16)
                     high.append(coarse)
                     low.append((bump - coarse.astype(jnp.float32)).astype(jnp.bfloat16))
-                stacked = jnp.concatenate(high + high + low, axis=0)
-                fields = jnp.dot(mix_ref[...], stacked, preferred_element_type=jnp.float32)
+                stacked = jnp.concatenate(high + low, axis=0)
+                both = jnp.dot(mix_ref[...], stacked, preferred_element_type=jnp.float32)
+                fields = both[:4 * STACK] + both[4 * STACK:]
                 after = []
                 for j in range(GROUPS):
                     red, green, blue, dense = (
@@ -180,7 +183,7 @@
         out_shape=[jax.ShapeDtypeStruct((capacity, 4, TILES, LANES), jnp.int16)] * tile_count,
         scratch_shapes=[
             pltpu.VMEM((KNOTS, 8, LANES), jnp.float32),
-            pltpu.VMEM((4 * STACK, 3 * KNOTS * STACK), jnp.bfloat16),
+            pltpu.VMEM((8 * STACK, 2 * KNOTS * STACK), jnp.bfloat16),
             pltpu.VMEM((tile_count // 8, 4, 8 * TILES, LANES), jnp.float32),
             pltpu.SMEM((tile_count,), jnp.int32),
         ],
@@ -195,12 +198,12 @@
         theirs = pl.multiple_of((2 * n + 1 - low) * row_share, row_share)
         for c in range(4):
             kept_ref[c, n * row_share:(n + 1) * row_share] = image[c, pl.ds(mine, row_share)]
-            given_ref[c, n * row_share:(n + 1) * row_share] = image[c, pl.ds(theirs, row_share)]
-
-
-def gather_kernel(tile_count, row_share, *refs):
+            given_ref[c, n * row_share:(n + 1) * row_share] = encode(image[c, pl.ds(theirs, row_share)])
+
+
+def gather_kernel(tile_count, row_share, last_bit, *refs):
     counts_ref, order_ref, flip_ref, me_ref, layer_ref, home_ref = refs[:6]
-    kept_ref, given_ref, brick_ref, image_ref, own_ref, own_sem = refs[5 + tile_count:]
+    kept_ref, given_ref, front_ref, brick_ref, image_ref, own_ref, own_sem = refs[5 + tile_count:]
     arrived = (own_ref,) + refs[6:5 + tile_count]
     own_copy = pltpu.make_async_copy(home_ref, own_ref, own_sem)
     own_copy.start()
@@ -253,19 +256,25 @@
                     line = moved if line is None else jnp.where(lane == bx, moved, line)
                 image_ref[c, pl.ds(by * BLOCK + s, TILES, stride=per_row), :] = line
     split_rows(image_ref, kept_ref, given_ref, layer_ref[0] & 1, row_share)
-
-
-def gather(counts, order, flip, me, layer, arrived, row_share):
+    front = (layer_ref[0] >> last_bit & 1) == flip_ref[me]
+    front_ref[...] = jnp.broadcast_to(jnp.where(front, 1.0, 0.0), (8, LANES))
+
+
+def gather(counts, order, flip, me, layer, arrived, row_share, last_bit):
     tile_count = counts.shape[0]
     scalar = pl.BlockSpec(memory_space=pltpu.SMEM)
     vmem = pl.BlockSpec(memory_space=pltpu.VMEM)
     rows, width = BY * BLOCK, BX * BLOCK
     half = jax.ShapeDtypeStruct((4, rows // 2, width), jnp.float32)
     return pl.pallas_call(
-        functools.partial(gather_kernel, tile_count, row_share),
+        functools.partial(gather_kernel, tile_count, row_share, last_bit),
         in_specs=[scalar] * 5 + [pl.BlockSpec(memory_space=pltpu.HBM)] + [vmem] * (tile_count - 1),
-        out_specs=[vmem] * 2,
-        out_shape=[half, half],
+        out_specs=[vmem] * 3,
+        out_shape=[
+            half,
+            jax.ShapeDtypeStruct(half.shape, jnp.int16),
+            jax.ShapeDtypeStruct((8, LANES), jnp.float32),
+        ],
         scratch_shapes=[
             pltpu.VMEM((DB * BY * BX, 4, TILES, LANES), jnp.float32),
             pltpu.VMEM((4, rows, width), jnp.float32),
@@ -274,48 +283,45 @@
         ],
         compiler_params=pltpu.CompilerParams(vmem_limit_bytes=GRANT),
         name="gather",
-    )(counts, order, flip, me, layer, *arrived)
+    )(counts, order, flip, me, layer, pltpu.with_memory_space_constraint(arrived[0], pltpu.HBM), *arrived[1:])
 
 
 def blend_kernel(bit, row_share, *refs):
-    flip_ref, me_ref, layer_ref, kept_ref, other_ref = refs[:5]
-    side = layer_ref[0] >> bit & 1
-    front = side == flip_ref[me_ref[0]]
-    last = len(refs) == 6
-    out_ref = refs[-1]
-
-    def blend(near_ref, far_ref):
-        uncovered = 1.0 - near_ref[3]
-        for c in range(4):
-            out_ref[c] = near_ref[c] + uncovered * far_ref[c]
-
-    @pl.when(front)
-    def _():
-        blend(kept_ref, other_ref)
-
-    @pl.when(jnp.logical_not(front))
-    def _():
-        blend(other_ref, kept_ref)
-
-    if not last:
-        split_rows(out_ref, refs[5], refs[6], layer_ref[0] >> (bit + 1) & 1, row_share)
+    flip_ref, me_ref, layer_ref, kept_ref, other_ref, kept_out, given_out, image_ref = refs
+    front = (layer_ref[0] >> bit & 1) == flip_ref[me_ref[0]]
+    kept_open = 1.0 - kept_ref[3]
+    other_open = 1.0 - decode(other_ref[3])
+    kept_part = jnp.where(front, 1.0, other_open)
+    other_part = jnp.where(front, kept_open, 1.0)
+    for c in range(4):
+        image_ref[c] = kept_part * kept_ref[c] + other_part * decode(other_ref[c])
+    split_rows(image_ref, kept_out, given_out, layer_ref[0] >> (bit + 1) & 1, row_share)
 
 
 def blend(flip, me, layer, kept, other, bit, row_share):
     scalar = pl.BlockSpec(memory_space=pltpu.SMEM)
     vmem = pl.BlockSpec(memory_space=pltpu.VMEM)
-    last = kept.shape[1] == row_share
-    whole = jax.ShapeDtypeStruct(kept.shape, jnp.float32)
-    half = jax.ShapeDtypeStruct((4, kept.shape[1] // 2, kept.shape[2]), jnp.float32)
+    half = (4, kept.shape[1] // 2, kept.shape[2])
     return pl.pallas_call(
         functools.partial(blend_kernel, bit, row_share),
         in_specs=[scalar] * 3 + [vmem] * 2,
-        out_specs=vmem if last else [vmem] * 2,
-        out_shape=whole if last else [half, half],
-        scratch_shapes=[] if last else [pltpu.VMEM(kept.shape, jnp.float32)],
+        out_specs=[vmem] * 2,
+        out_shape=[
+            jax.ShapeDtypeStruct(half, jnp.float32),
+            jax.ShapeDtypeStruct(half, jnp.int16),
+        ],
+        scratch_shapes=[pltpu.VMEM(kept.shape, jnp.float32)],
         compiler_params=pltpu.CompilerParams(vmem_limit_bytes=GRANT),
         name="blend",
     )(flip, me, layer, kept, other)
+
+
+def last_blend(front, kept, coded):
+    other = decode(coded)
+    front = front[:1][None] > 0.5
+    kept_part = jnp.where(front, 1.0, 1.0 - other[3:])
+    other_part = jnp.where(front, 1.0 - kept[3:], 1.0)
+    return kept_part * kept + other_part * other
 
 
 def swapped(block, axis, bit):
@@ -336,14 +342,14 @@
         route = [(i, (i + r) % tile_count) for i in range(tile_count)]
         arrived.append(lax.ppermute(sent[r], "tile", route))
     row_share = BY * BLOCK // depth_count
-    kept, given = gather(counts, order, view_flip, me, layer, arrived, row_share)
     levels = depth_count.bit_length() - 1
-    for bit in range(levels):
+    kept, given, front = gather(
+        counts, order, view_flip, me, layer, arrived, row_share, levels - 1
+    )
+    for bit in range(levels - 1):
         other = swapped(given, "depth", bit)
-        blended = blend(view_flip, me, layer, kept, other, bit, row_share)
-        if bit < levels - 1:
-            kept, given = blended
-    return blended
+        kept, given = blend(view_flip, me, layer, kept, other, bit, row_share)
+    return last_blend(front, kept, swapped(given, "depth", levels - 1))
 
 
 def solution(mesh):

time: 55.3 us -> 54 us (0.976)
  Pallas kernels: 12.5 us -> 22.9 us
  starting transfers between devices: 32.5 us -> 23.3 us
  waiting for transfers between devices: 8.81 us -> 6.3 us
  local copies, waits for them, and re-layouts: 0.85 us -> 0.01 us
  other arithmetic: 0 us -> 0.7 us
    pallas_call x1, Pallas kernels: 9.27 us -> 20.5 us  [march(): pl.pallas_call(functools.partial(march_kernel, step_size, tile_count, til...]
    ppermute x7, starting transfers between devices: 31.9 us -> 21 us  [body(): arrived.append(lax.ppermute(sent[r], 'tile', route))]
    ppermute x2, waiting for transfers between devices: 5.14 us -> 3.13 us  [swapped(): return lax.ppermute(block, axis, [(i, i ^ 1 << bit) for i in range(count)])]
    ppermute x2, starting transfers between devices: 0.6 us -> 2.32 us  [swapped(): return lax.ppermute(block, axis, [(i, i ^ 1 << bit) for i in range(count)])]
    pallas_call x2 -> x1, Pallas kernels: 1.77 us -> 0.63 us  [blend(): pl.pallas_call(functools.partial(blend_kernel, bit, row_share), in_specs=...]
    unnamed x8 -> x6, local copies, waits for them, and re-layouts: 0.85 us -> 0.01 us
    add x0 -> x1, other arithmetic: none -> 0.66 us  [last_blend(): return kept_part * kept + other_part * other]
  transfers between devices with their start and end apart: 9 -> 9, of which waited for: 6 -> 4; matrix products, arithmetic and copies ran while one was open for 0% -> 0% of each run, Pallas kernels for 0% -> 0%
where the time goes in v5:
time: 54 us; the launch traced here: 53.3 us
  starting transfers between devices  23.3 us (43%)
  Pallas kernels  22.9 us (42%)
  waiting for transfers between devices  6.3 us (12%)
  other arithmetic  0.7 us (1%)
    ppermute x7, starting transfers between devices, body(): arrived.append(lax.ppermute(sent[r], 'tile', route))  21 us
    pallas_call x1, Pallas kernels, march(): pl.pallas_call(functools.partial(march_kernel, step_size, tile_count, til...  20.5 us
    ppermute x7, waiting for transfers between devices, body(): arrived.append(lax.ppermute(sent[r], 'tile', route))  3.17 us
    ppermute x2, waiting for transfers between devices, swapped(): return lax.ppermute(block, axis, [(i, i ^ 1 << bit) for i in range(count)])  3.13 us
    ppermute x2, starting transfers between devices, swapped(): return lax.ppermute(block, axis, [(i, i ^ 1 << bit) for i in range(count)])  2.32 us
    pallas_call x1, Pallas kernels, gather(): pl.pallas_call(functools.partial(gather_kernel, tile_count, row_share, la...  1.78 us
  transfers between devices with their start and end apart: 9, of which 4 were waited for; matrix products, arithmetic and copies ran while one was open for 0% of the time, Pallas kernels for 0%

profile of v5, /device:TPU:0, one launch (start us, length us, event | category | flops | bytes accessed | tf_op | source)
XLA Modules:
  0.0 53.3 jit_solution(13546165722795555578)
XLA Ops:
  0.0 0.0 copy-start
  0.0 0.0 copy-start.2
  0.0 0.0 copy-start.1
  0.0 20.5 %march.1 = (s16[8,4,8,128]{3,2,1,0:T(8,128)(2,1)}, s16[8,4,8,128]{3,2,1,0:T(8,128)(2,1)}, s16[8,4,8,128]{3,2,1,0:T(8,128)(2,1)}, s16[8,4,8,128]{3,2,1,0:T(8,128)...) custom-call(s32[8]{0:T(128)} %bitcast.12, ...), custom_call_target="tpu_custom_call" | custom-call | tf_op jit(solution)/shard_map/march/pallas_call | solution.py:174
  20.5 8.2 %collective-permute-start = (s16[8,4,8,128]{3,2,1,0:T(8,128)(2,1)}, s16[8,4,8,128]{3,2,1,0:T(8,128)(2,1)S(1)}, u32[]{:S(2)}, u32[]{:S(2)}) collective-permute-start(s16[8,4,8,128]{3,2,1,0:T(8,128)(2,1)} %get-tuple-element.19), channel_id=1, source_target_pairs={{0,4},{4,8},{8,12},{12,16},{16,20},{20,24},{24,28},{28,0},{1,5},{5... | collective-permute-start | bytes 196616 | tf_op jit(solution)/shard_map/ppermute | solution.py:343
  28.8 0.0 collective-permute-start.1
  28.8 7.4 %collective-permute-start.2 = (s16[8,4,8,128]{3,2,1,0:T(8,128)(2,1)}, s16[8,4,8,128]{3,2,1,0:T(8,128)(2,1)S(1)}, u32[]{:S(2)}, u32[]{:S(2)}) collective-permute-start(s16[8,4,8,128]{3,2,1,0:T(8,128)(2,1)} %get-tuple-element.21), channel_id=1, source_target_pairs={{0,12},{4,16},{8,20},{12,24},{16,28},{20,0},{24,4},{28,8},{1,13},{... | collective-permute-start | bytes 196616 | tf_op jit(solution)/shard_map/ppermute | solution.py:343
  36.2 0.0 collective-permute-start.3
  36.2 2.4 %collective-permute-start.4 = (s16[8,4,8,128]{3,2,1,0:T(8,128)(2,1)}, s16[8,4,8,128]{3,2,1,0:T(8,128)(2,1)S(1)}, u32[]{:S(2)}, u32[]{:S(2)}) collective-permute-start(s16[8,4,8,128]{3,2,1,0:T(8,128)(2,1)} %get-tuple-element.23), channel_id=1, source_target_pairs={{0,20},{4,24},{8,28},{12,0},{16,4},{20,8},{24,12},{28,16},{1,21},{... | collective-permute-start | bytes 196616 | tf_op jit(solution)/shard_map/ppermute | solution.py:343
  38.6 0.0 collective-permute-done.refs_6_
  38.6 0.9 %collective-permute-start.5 = (s16[8,4,8,128]{3,2,1,0:T(8,128)(2,1)}, s16[8,4,8,128]{3,2,1,0:T(8,128)(2,1)S(1)}, u32[]{:S(2)}, u32[]{:S(2)}) collective-permute-start(s16[8,4,8,128]{3,2,1,0:T(8,128)(2,1)} %get-tuple-element.24), channel_id=1, source_target_pairs={{0,24},{4,28},{8,0},{12,4},{16,8},{20,12},{24,16},{28,20},{1,25},{... | collective-permute-start | bytes 196616 | tf_op jit(solution)/shard_map/ppermute | solution.py:343
  39.5 0.0 collective-permute-done.1.refs_7_
  39.5 2.0 %collective-permute-start.6 = (s16[8,4,8,128]{3,2,1,0:T(8,128)(2,1)}, s16[8,4,8,128]{3,2,1,0:T(8,128)(2,1)S(1)}, u32[]{:S(2)}, u32[]{:S(2)}) collective-permute-start(s16[8,4,8,128]{3,2,1,0:T(8,128)(2,1)} %get-tuple-element.25), channel_id=1, source_target_pairs={{0,28},{4,0},{8,4},{12,8},{16,12},{20,16},{24,20},{28,24},{1,29},{... | collective-permute-start | bytes 196616 | tf_op jit(solution)/shard_map/ppermute | solution.py:343
  41.5 0.0 collective-permute-done.2.refs_8_
  41.5 1.8 %collective-permute-done.3.refs_9_ = s16[8,4,8,128]{3,2,1,0:T(8,128)(2,1)S(1)} collective-permute-done((s16[8,4,8,128]{3,2,1,0:T(8,128)(2,1)}, s16[8,4,8,128]{3,2,1,0:T(8,128)(2,1)S(1)}, u32[]{:S(2)}, u32[]{:S(2)}) %collective-permute-start.3) | collective-permute-done | bytes 65568 | tf_op jit(solution)/shard_map/ppermute | solution.py:343
  43.4 0.0 collective-permute-done.4.refs_10_
  43.4 1.3 %collective-permute-done.5.refs_11_ = s16[8,4,8,128]{3,2,1,0:T(8,128)(2,1)S(1)} collective-permute-done((s16[8,4,8,128]{3,2,1,0:T(8,128)(2,1)}, s16[8,4,8,128]{3,2,1,0:T(8,128)(2,1)S(1)}, u32[]{:S(2)}, u32[]{:S(2)}) %collective-permute-start.5) | collective-permute-done | bytes 65568 | tf_op jit(solution)/shard_map/ppermute | solution.py:343
  44.7 0.0 collective-permute-done.6.refs_12_
  44.7 0.0 copy-done
  44.7 0.0 copy-done.2
  44.7 0.0 copy-done.1
  44.7 1.8 %gather.1 = (f32[4,64,128]{2,1,0:T(8,128)S(1)}, s16[4,64,128]{2,1,0:T(8,128)(2,1)S(1)}, f32[8,128]{1,0:T(8,128)S(1)}) custom-call(s32[8]{0:T(128)S(1)} %bitcast.13, s32[8]{0:T(128)S(1)} %bitcast.15, s32[8]{0:T(128)S(1)} %copy-done, s32[1]{0:T(128)} %bitcast.2.refs_3_.refs_1_, s32[1]{0:T(128)} %bitcast.3.refs_4_.refs_2_, ...), custom_call_target="tpu_custom_call" | custom-call | tf_op jit(solution)/shard_map/gather/pallas_call | solution.py:269
  46.5 0.1 collective-permute-start.7
  46.6 1.2 %collective-permute-done.7.refs_4_ = s16[4,64,128]{2,1,0:T(8,128)(2,1)S(1)} collective-permute-done((s16[4,64,128]{2,1,0:T(8,128)(2,1)S(1)}, s16[4,64,128]{2,1,0:T(8,128)(2,1)S(1)}, u32[]{:S(2)}, u32[]{:S(2)}) %collective-permute-start.7) | collective-permute-done | bytes 65568 | tf_op jit(solution)/shard_map/ppermute | solution.py:329
  47.8 0.6 %blend.1 = (f32[4,32,128]{2,1,0:T(8,128)S(1)}, s16[4,32,128]{2,1,0:T(8,128)(2,1)S(1)}) custom-call(s32[8]{0:T(128)S(1)} %copy-done, s32[1]{0:T(128)} %bitcast.2.refs_3_.refs_1_, s32[1]{0:T(128)} %bitcast.3.refs_4_.refs_2_, f32[4,64,128]{2,1,0:T(8,128)S(1)} %get-tuple-element.27.refs_3_, s16[4,64,128]{2,1,0:T(8,128)(2,1)S(1)} %collective-permute-done.7.refs_4_), custom_call_target="tpu_custom_call" | custom-call | tf_op jit(solution)/shard_map/blend/pallas_call | solution.py:305
  48.5 2.2 %collective-permute-start.8 = (s16[4,32,128]{2,1,0:T(8,128)(2,1)S(1)}, s16[4,32,128]{2,1,0:T(8,128)(2,1)S(1)}, u32[]{:S(2)}, u32[]{:S(2)}) collective-permute-start(s16[4,32,128]{2,1,0:T(8,128)(2,1)S(1)} %get-tuple-element.29), channel_id=1, source_target_pairs={{0,2},{1,3},{2,0},{3,1},{4,6},{5,7},{6,4},{7,5},{8,10},{9,11},{10,... | collective-permute-start | bytes 98312 | tf_op jit(solution)/shard_map/ppermute | solution.py:329
  50.7 1.9 %collective-permute-done.8 = s16[4,32,128]{2,1,0:T(8,128)(2,1)S(1)} collective-permute-done((s16[4,32,128]{2,1,0:T(8,128)(2,1)S(1)}, s16[4,32,128]{2,1,0:T(8,128)(2,1)S(1)}, u32[]{:S(2)}, u32[]{:S(2)}) %collective-permute-start.8) | collective-permute-done | bytes 32800 | tf_op jit(solution)/shard_map/ppermute | solution.py:329
  52.6 0.7 %multiply_add_fusion = f32[4,32,128]{2,1,0:T(8,128)} fusion(f32[4,32,128]{2,1,0:T(8,128)S(1)} %get-tuple-element.30, f32[32,128]{1,0:T(8,128)S(1)} %get-tuple-element.32, f32[32,128]{1,0:T(8,128)S(1)} %get-tuple-element.31, s16[4,32,128]{2,1,0:T(8,128)(2,1)S(1)} %collective-permute-done.8), kind=kLoop, calls=%fused_computation | loop fusion | flops 147456 | bytes 196608 | tf_op jit(solution)/shard_map/add | solution.py:324
  (3 shorter events, 0.0 us)
Async XLA Ops:
  0.0 44.7 %copy-start = (s32[8]{0:T(128)S(1)}, s32[8]{0:T(128)}, u32[]{:S(2)}) copy-start(s32[8]{0:T(128)} %refs_0_.1) | copy-start | bytes 100
  0.0 44.7 %copy-start.2 = (s32[1,8]{1,0:T(1,128)S(1)}, s32[1,8]{1,0:T(1,128)}, u32[]{:S(2)}) copy-start(s32[1,8]{1,0:T(1,128)} %param.8) | copy-start | bytes 100
  0.0 44.7 %copy-start.1 = (s32[1,8]{1,0:T(1,128)S(1)}, s32[1,8]{1,0:T(1,128)}, u32[]{:S(2)}) copy-start(s32[1,8]{1,0:T(1,128)} %param.7) | copy-start | bytes 100
  20.5 18.1 %collective-permute-start = (s16[8,4,8,128]{3,2,1,0:T(8,128)(2,1)}, s16[8,4,8,128]{3,2,1,0:T(8,128)(2,1)S(1)}, u32[]{:S(2)}, u32[]{:S(2)}) collective-permute-start(s16[8,4,8,128]{3,2,1,0:T(8,128)(2,1)} %get-tuple-element.19), channel_id=1, source_target_pairs={{0,4},{4,8},{8,12},{12,16},{16,20},{20,24},{24,28},{28,0},{1,5},{5... | collective-permute-start | bytes 196616 | tf_op jit(solution)/shard_map/ppermute | solution.py:343
  28.8 10.8 %collective-permute-start.1 = (s16[8,4,8,128]{3,2,1,0:T(8,128)(2,1)}, s16[8,4,8,128]{3,2,1,0:T(8,128)(2,1)S(1)}, u32[]{:S(2)}, u32[]{:S(2)}) collective-permute-start(s16[8,4,8,128]{3,2,1,0:T(8,128)(2,1)} %get-tuple-element.20), channel_id=1, source_target_pairs={{0,8},{4,12},{8,16},{12,20},{16,24},{20,28},{24,0},{28,4},{1,9},{5... | collective-permute-start | bytes 196616 | tf_op jit(solution)/shard_map/ppermute | solution.py:343
  28.8 12.8 %collective-permute-start.2 = (s16[8,4,8,128]{3,2,1,0:T(8,128)(2,1)}, s16[8,4,8,128]{3,2,1,0:T(8,128)(2,1)S(1)}, u32[]{:S(2)}, u32[]{:S(2)}) collective-permute-start(s16[8,4,8,128]{3,2,1,0:T(8,128)(2,1)} %get-tuple-element.21), channel_id=1, source_target_pairs={{0,12},{4,16},{8,20},{12,24},{16,28},{20,0},{24,4},{28,8},{1,13},{... | collective-permute-start | bytes 196616 | tf_op jit(solution)/shard_map/ppermute | solution.py:343
  36.2 7.2 %collective-permute-start.3 = (s16[8,4,8,128]{3,2,1,0:T(8,128)(2,1)}, s16[8,4,8,128]{3,2,1,0:T(8,128)(2,1)S(1)}, u32[]{:S(2)}, u32[]{:S(2)}) collective-permute-start(s16[8,4,8,128]{3,2,1,0:T(8,128)(2,1)} %get-tuple-element.22), channel_id=1, source_target_pairs={{0,16},{4,20},{8,24},{12,28},{16,0},{20,4},{24,8},{28,12},{1,17},{... | collective-permute-start | bytes 196616 | tf_op jit(solution)/shard_map/ppermute | solution.py:343
  36.2 7.2 %collective-permute-start.4 = (s16[8,4,8,128]{3,2,1,0:T(8,128)(2,1)}, s16[8,4,8,128]{3,2,1,0:T(8,128)(2,1)S(1)}, u32[]{:S(2)}, u32[]{:S(2)}) collective-permute-start(s16[8,4,8,128]{3,2,1,0:T(8,128)(2,1)} %get-tuple-element.23), channel_id=1, source_target_pairs={{0,20},{4,24},{8,28},{12,0},{16,4},{20,8},{24,12},{28,16},{1,21},{... | collective-permute-start | bytes 196616 | tf_op jit(solution)/shard_map/ppermute | solution.py:343
  38.6 6.1 %collective-permute-start.5 = (s16[8,4,8,128]{3,2,1,0:T(8,128)(2,1)}, s16[8,4,8,128]{3,2,1,0:T(8,128)(2,1)S(1)}, u32[]{:S(2)}, u32[]{:S(2)}) collective-permute-start(s16[8,4,8,128]{3,2,1,0:T(8,128)(2,1)} %get-tuple-element.24), channel_id=1, source_target_pairs={{0,24},{4,28},{8,0},{12,4},{16,8},{20,12},{24,16},{28,20},{1,25},{... | collective-permute-start | bytes 196616 | tf_op jit(solution)/shard_map/ppermute | solution.py:343
  39.5 5.2 %collective-permute-start.6 = (s16[8,4,8,128]{3,2,1,0:T(8,128)(2,1)}, s16[8,4,8,128]{3,2,1,0:T(8,128)(2,1)S(1)}, u32[]{:S(2)}, u32[]{:S(2)}) collective-permute-start(s16[8,4,8,128]{3,2,1,0:T(8,128)(2,1)} %get-tuple-element.25), channel_id=1, source_target_pairs={{0,28},{4,0},{8,4},{12,8},{16,12},{20,16},{24,20},{28,24},{1,29},{... | collective-permute-start | bytes 196616 | tf_op jit(solution)/shard_map/ppermute | solution.py:343
  46.5 1.3 %collective-permute-start.7 = (s16[4,64,128]{2,1,0:T(8,128)(2,1)S(1)}, s16[4,64,128]{2,1,0:T(8,128)(2,1)S(1)}, u32[]{:S(2)}, u32[]{:S(2)}) collective-permute-start(s16[4,64,128]{2,1,0:T(8,128)(2,1)S(1)} %get-tuple-element.28), channel_id=1, source_target_pairs={{0,1},{1,0},{2,3},{3,2},{4,5},{5,4},{6,7},{7,6},{8,9},{9,8},{10,11... | collective-permute-start | bytes 196616 | tf_op jit(solution)/shard_map/ppermute | solution.py:329
  48.5 4.1 %collective-permute-start.8 = (s16[4,32,128]{2,1,0:T(8,128)(2,1)S(1)}, s16[4,32,128]{2,1,0:T(8,128)(2,1)S(1)}, u32[]{:S(2)}, u32[]{:S(2)}) collective-permute-start(s16[4,32,128]{2,1,0:T(8,128)(2,1)S(1)} %get-tuple-element.29), channel_id=1, source_target_pairs={{0,2},{1,3},{2,0},{3,1},{4,6},{5,7},{6,4},{7,5},{8,10},{9,11},{10,... | collective-permute-start | bytes 98312 | tf_op jit(solution)/shard_map/ppermute | solution.py:329
